TPU v7x, 32 devices: a whole 2x2x4 slice. The times are simulated.
32 devices in a mesh: gx: 4 (over y, core), gy: 4 (over z), gz: 2 (over x).
Axes of the slice: x: 2, y: 2, z: 4, core: 2. Of those that a mesh axis runs over, the one named last changes fastest.
Arguments:
- orbital_values: bfloat16 [64, 64, 48, 384], P('gx', 'gy', 'gz'), may hold values from -6 to 6
- dm_slabs: bfloat16 [1536, 8, 384], P(('gx', 'gy', 'gz')), may hold values from -0.015625 to 0.015625
- slab_tile: int32 [1536], P(('gx', 'gy', 'gz')), may hold values from 0 to 15, as said below
- slab_place: int32 [1536], P(('gx', 'gy', 'gz')), may hold values from 0 to 47, as said below
Outputs:
- potential: float32 [64, 64, 48], P('gx', 'gy', 'gz')
- pot_slabs: bfloat16 [1536, 8, 384], P(('gx', 'gy', 'gz'))
Inputs may be any that keep to these rules, and one draw needn't show every extreme that they name: `slab_tile`: within each layer along gz, every tile of that layer has exactly one slab for each place 0 .. 47, held by devices of the same layer; no device holds more than 6 slabs of one tile, and in every layer some device holds exactly 6 slabs of some tile. See slab_tile: the pair (slab_tile, slab_place) is different for all slabs of one layer.
All inputs are finite; a program needn't handle non-finite values.
Results may differ from a plain program's by a relative error of at most 0.0023.
Values may be sent and summed in bfloat16 or wider, within the bound.
No kernel may reach another device: no remote copies, remote signals or barrier semaphores. Data moves between devices by JAX's collectives and lax.ppermute only.
A program may use at most 64 MiB of HBM per device.

v0:
```python
import functools
import math

import jax
import jax.numpy as jnp
import numpy as np
from jax import lax
from jax.experimental import pallas as pl
from jax.experimental.pallas import tpu as pltpu
from jax.sharding import PartitionSpec as P


RADIUS = 8
LANES = 128

ALPHAS = (0.012, 0.025, 0.05, 0.1, 0.2, 0.4, 0.8, 1.6)
MIXES = (0.3, 0.3, 0.32, 0.34, 0.36, 0.38, 0.4, 0.42)

VMEM_SPEC = pl.BlockSpec(memory_space=pltpu.VMEM)
SMEM_SPEC = pl.BlockSpec(memory_space=pltpu.SMEM)
HBM_SPEC = pl.BlockSpec(memory_space=pltpu.HBM)


def in_hbm(array):
    return pltpu.with_memory_space_constraint(array, pltpu.HBM)


def grant(mebibytes):
    return pltpu.CompilerParams(vmem_limit_bytes=mebibytes << 20)


def kernel_tables(radius):
    tap_table = [
        [math.exp(-alpha * offset * offset) for offset in range(-radius, radius + 1)]
        for alpha in ALPHAS
    ]
    mix = [
        MIXES[term] / sum((tap * tap for tap in tap_table[term])) ** 1.5
        for term in range(len(ALPHAS))
    ]
    return (tap_table, mix)


def cost(flops, moved_bytes):
    return pl.CostEstimate(flops=flops, bytes_accessed=moved_bytes, transcendentals=0)


def for_each_slab(tile_ref, count_ref, tile_count, slab_count, visit):
    for t in range(tile_count):
        count_ref[t] = 0

    def step(i, carry):
        t = tile_ref[i]
        slot = count_ref[t]
        count_ref[t] = slot + 1
        visit(i, t, slot)
        return carry

    lax.fori_loop(0, slab_count, step, 0, unroll=4)


def pack_kernel(
    capacity, chunks, empty, tile_hbm, place_hbm, slab_hbm, out_ref,
    tile_ref, place_ref, slab_ref, count_ref, label_ref, sems,
):
    copies = [
        pltpu.make_async_copy(tile_hbm, tile_ref, sems.at[0]),
        pltpu.make_async_copy(place_hbm, place_ref, sems.at[1]),
        pltpu.make_async_copy(slab_hbm, slab_ref, sems.at[2]),
    ]
    for copy in copies:
        copy.start()
    tile_count = out_ref.shape[0]
    label_ref[...] = jnp.full(label_ref.shape, empty, jnp.float32)
    out_ref[...] = jnp.zeros(out_ref.shape, out_ref.dtype)
    for copy in copies:
        copy.wait()

    def visit(i, t, slot):
        slab = slab_ref[i]
        for c in range(chunks):
            out_ref[t, slot * chunks + c] = slab[:, c * LANES : (c + 1) * LANES]
        label = place_ref[i].astype(jnp.float32)
        label_ref[t, pl.ds(slot, 1), :] = jnp.full((1, LANES), label, jnp.float32)

    for_each_slab(tile_ref, count_ref, tile_count, slab_ref.shape[0], visit)
    out_ref[:, capacity * chunks] = label_ref[...].astype(jnp.bfloat16)


def odd_row():
    return lax.rem(lax.axis_index("gy"), 2)


def turn_kernel(planes, values_hbm, near_ref, far_hbm, values_ref, far_ref, sems, out_sem):
    points = values_ref.shape[0]
    plane = points // planes
    half = plane // 2
    copies = []
    for x in range(0, planes, 2):
        part = slice(x * plane, (x + 2) * plane)
        copies.append(
            pltpu.make_async_copy(values_hbm.at[part], values_ref.at[part], sems.at[x // 2])
        )
        copies[-1].start()
    near_start = odd_row() * half
    for x in range(0, planes, 2):
        copies[x // 2].wait()
        for start, out_ref in ((near_start, near_ref), (half - near_start, far_ref)):
            rows = [
                values_ref[pl.ds(pl.multiple_of((x + i) * plane + start, half), half), :]
                for i in range(2)
            ]
            out_ref[:, x * half : (x + 2) * half] = jnp.concatenate(rows, axis=0).T
    copy = pltpu.make_async_copy(far_ref, far_hbm, out_sem.at[0])
    copy.start()
    copy.wait()


def arrange(capacity, chunks, arrived_ref, place_ref, wide_ref, turned_ref):
    tile_count, _, rows, _ = arrived_ref.shape
    slots = tile_count * capacity
    labels = arrived_ref[:, capacity * chunks].astype(jnp.float32)[:, :capacity]
    labels = labels.reshape(slots, LANES)
    width = place_ref.shape[1]
    for g in range(width // LANES):
        group = labels[g * LANES : (g + 1) * LANES]
        here = lax.broadcasted_iota(jnp.int32, group.shape, 0) == lax.broadcasted_iota(
            jnp.int32, group.shape, 1
        )
        place_ref[:, g * LANES : (g + 1) * LANES] = jnp.sum(
            jnp.where(here, group, 0.0), axis=0, keepdims=True
        ).astype(jnp.int32)
    first_row = jnp.broadcast_to(labels.reshape(slots, 1, LANES) * rows, (slots, rows, LANES))
    source = first_row + lax.broadcasted_iota(jnp.int32, (slots, rows, LANES), 1).astype(
        jnp.float32
    )
    lane = lax.broadcasted_iota(jnp.int32, (slots, rows, LANES), 2).astype(jnp.float32)
    hot = []
    for c in range(chunks):
        match = jnp.where(source == lane + float(c * LANES), 1.0, 0.0)
        hot.append(match.reshape(slots * rows, LANES).astype(jnp.bfloat16))
    hot = jnp.concatenate(hot, axis=1)
    for c in range(chunks):
        for t in range(tile_count):
            for k in range(capacity):
                row = (t * capacity + k) * rows
                wide_ref[row : row + rows, :] = arrived_ref[t, k * chunks + c].astype(jnp.float32)
        across = wide_ref[...].T.astype(jnp.bfloat16)
        turned_ref[c * LANES : (c + 1) * LANES, :] = jnp.dot(
            across, hot, preferred_element_type=jnp.float32
        ).astype(jnp.bfloat16)


def half_density(piece, turned_ref, values_ref, out_ref):
    half = out_ref.shape[1]
    for q in range(values_ref.shape[1] // piece):
        block = values_ref[:, q * piece : (q + 1) * piece]
        mixed = jnp.dot(turned_ref[...], block, preferred_element_type=jnp.float32)
        density = jnp.sum(mixed * block.astype(jnp.float32), axis=0, keepdims=True)
        for p in range(piece // half):
            row = q * (piece // half) + p
            out_ref[row : row + 1, :] = density[:, p * half : (p + 1) * half]


def near_kernel(
    capacity, chunks, piece, arrived_ref, near_ref, far_hbm,
    out_ref, place_ref, turned_ref, far_ref, wide_ref, sem,
):
    copy = pltpu.make_async_copy(far_hbm, far_ref, sem.at[0])
    copy.start()
    arrange(capacity, chunks, arrived_ref, place_ref, wide_ref, turned_ref)
    half_density(piece, turned_ref, near_ref, out_ref)
    copy.wait()


def far_kernel(piece, turned_ref, far_ref, out_ref):
    half_density(piece, turned_ref, far_ref, out_ref)


def join_kernel(near_ref, far_ref, wrap_ref, pair_ref, out_ref, top_ref, bottom_ref):
    half = near_ref.shape[1]
    odd = odd_row() == 1
    blocks = (
        jnp.where(odd, pair_ref[...], wrap_ref[...]),
        jnp.where(odd, far_ref[...], near_ref[...]),
        jnp.where(odd, near_ref[...], far_ref[...]),
        jnp.where(odd, wrap_ref[...], pair_ref[...]),
    )
    for i, block in enumerate(blocks):
        out_ref[:, i * half : (i + 1) * half] = block
    top_ref[...] = out_ref[: top_ref.shape[0], :]
    bottom_ref[...] = out_ref[out_ref.shape[0] - bottom_ref.shape[0] :, :]


def split_dot(left, high, low):
    left_high = left.astype(jnp.bfloat16)
    left_low = (left - left_high.astype(jnp.float32)).astype(jnp.bfloat16)
    out = jnp.dot(left_high, high, preferred_element_type=jnp.float32)
    out = out + jnp.dot(left_low, high, preferred_element_type=jnp.float32)
    return out + jnp.dot(left_high, low, preferred_element_type=jnp.float32)


def filter_kernel(parts, *refs):
    taps_ref, band_high, band_low, fold_high, fold_low = refs[:5]
    blocks = refs[5 : 5 + 3 * parts]
    out_ref, field_ref, grid_ref, first_ref, second_ref, third_ref = refs[5 + 3 * parts :]
    size_x, size_y, size_z = out_ref.shape
    wide_y, wide_x, lanes = first_ref.shape
    for part in range(parts):
        start = 0
        for block in blocks[3 * part : 3 * part + 3]:
            rows = block.shape[0]
            for y in range(wide_y):
                grid_ref[y, start : start + rows, part * size_z : (part + 1) * size_z] = block[
                    :, y * size_z : (y + 1) * size_z
                ]
            start += rows
    grid = grid_ref[...].reshape(wide_y * wide_x, parts * size_z)
    first_ref[...] = split_dot(grid, band_high[...], band_low[...]).reshape(wide_y, wide_x, lanes)

    def tap(distance, rows):
        return jnp.broadcast_to(taps_ref[distance : distance + 1, :], (rows, lanes))

    def smooth(y, carry):
        run = tap(0, wide_x) * first_ref[y + RADIUS]
        for d in range(1, RADIUS + 1):
            pair = first_ref[y + (RADIUS - d)] + first_ref[y + (RADIUS + d)]
            run = run + tap(d, wide_x) * pair
        second_ref[y] = run
        run = tap(0, size_x) * second_ref[y, RADIUS : RADIUS + size_x, :]
        for d in range(1, RADIUS + 1):
            pair = (
                second_ref[y, RADIUS - d : RADIUS - d + size_x, :]
                + second_ref[y, RADIUS + d : RADIUS + d + size_x, :]
            )
            run = run + tap(d, size_x) * pair
        third_ref[y] = run
        return carry

    lax.fori_loop(0, size_y, smooth, 0, unroll=4)
    filtered = third_ref[...].reshape(size_y * size_x, lanes)
    folded = split_dot(filtered, fold_high[...], fold_low[...]).reshape(size_y, size_x, size_z)
    for y in range(size_y):
        out_ref[:, y, :] = folded[y]
        field_ref[:, y * size_z : (y + 1) * size_z] = folded[y]


def potential_kernel(
    capacity, chunks, rows, weight, piece, place_vmem, field_ref, near_ref, far_ref,
    out_ref, total_ref, place_ref, sem,
):
    copy = pltpu.make_async_copy(place_vmem, place_ref, sem.at[0])
    copy.start()
    list_orb, points = near_ref.shape
    half = field_ref.shape[1] // 2
    odd = odd_row() == 1
    low, high = field_ref[:, :half] * weight, field_ref[:, half:] * weight
    first = True
    for values_ref, source in (
        (near_ref, jnp.where(odd, high, low)),
        (far_ref, jnp.where(odd, low, high)),
    ):
        for q in range(points // piece):
            field = jnp.concatenate(
                [
                    source[x : x + 1, :]
                    for x in range(q * piece // half, (q + 1) * piece // half)
                ],
                axis=1,
            )
            block = values_ref[:, q * piece : (q + 1) * piece]
            weighted = (field * block.astype(jnp.float32)).astype(jnp.bfloat16)
            term = lax.dot_general(
                block, weighted, (((1,), (1,)), ((), ())), preferred_element_type=jnp.float32
            )
            total_ref[...] = term if first else total_ref[...] + term
            first = False

    copy.wait()
    last = list_orb // rows - 1

    def visit(j, carry):
        t, k = j // capacity, j % capacity
        row = pl.multiple_of(jnp.minimum(place_ref[0, j], last) * rows, rows)
        for c in range(chunks):
            lanes = slice(c * LANES, (c + 1) * LANES)
            out_ref[t, k, :, lanes] = total_ref[pl.ds(row, rows), lanes].astype(jnp.bfloat16)
        return carry

    lax.fori_loop(0, out_ref.shape[0] * capacity, visit, 0, unroll=4)


def write_kernel(grid_ref, grid_hbm, sem):
    copy = pltpu.make_async_copy(grid_ref, grid_hbm, sem.at[0])
    copy.start()
    copy.wait()


def unpack_kernel(tile_count, tile_ref, back_ref, out_hbm, count_ref, sem):
    def visit(i, t, slot):
        pltpu.make_async_copy(back_ref.at[t, slot], out_hbm.at[i], sem.at[0]).start()

    for_each_slab(tile_ref, count_ref, tile_count, out_hbm.shape[0], visit)
    pltpu.make_async_copy(out_hbm, out_hbm, sem.at[0]).wait()


def moved(block, shifts):
    axes = tuple(shifts)
    sizes = [lax.axis_size(axis) for axis in axes]
    pairs = []
    for source in np.ndindex(*sizes):
        target = [(s + shifts[axis]) % n for s, axis, n in zip(source, axes, sizes)]
        pairs.append(
            (int(np.ravel_multi_index(source, sizes)), int(np.ravel_multi_index(target, sizes)))
        )
    return lax.ppermute(block, axes, pairs)


def band_tables(size_z, neighbours):
    tap_table, mix = kernel_tables(RADIUS)

    def band(shift):
        table = np.zeros((size_z, len(ALPHAS), size_z), np.float64)
        for m in range(len(ALPHAS)):
            for source in range(size_z):
                for target in range(size_z):
                    offset = source + shift - target
                    if abs(offset) <= RADIUS:
                        table[source, m, target] = tap_table[m][offset + RADIUS]
        return table.reshape(size_z, len(ALPHAS) * size_z)

    own, low, high = band(0), band(-size_z), band(size_z)
    bands = {0: [own + low + high], 1: [own, low + high], 2: [own, low, high]}[neighbours]
    taps = np.zeros((16, len(ALPHAS) * size_z), np.float64)
    for d in range(RADIUS + 1):
        taps[d] = np.repeat([row[RADIUS + d] for row in tap_table], size_z)
    fold = np.concatenate([mix[m] * np.eye(size_z) for m in range(len(ALPHAS))], axis=0)

    def split(table):
        high = table.astype(np.float32).astype(jnp.bfloat16)
        low = (table - high.astype(np.float64)).astype(np.float32).astype(jnp.bfloat16)
        return [high, low]

    return [taps.astype(np.float32), *split(np.concatenate(bands, axis=0)), *split(fold)]


def local(orbital_values, dm_slabs, slab_tile, slab_place):
    size_x, size_y, size_z, list_orb = orbital_values.shape
    slab_count, atom_orb, _ = dm_slabs.shape
    list_blk = list_orb // atom_orb
    tile_count = lax.axis_size("gx") * lax.axis_size("gy")
    capacity = max(2, 2 * ((list_blk + tile_count - 1) // tile_count))
    chunks = list_orb // LANES
    tile_points = size_x * size_y * size_z
    plane = size_y * size_z
    counts = pltpu.SMEM((tile_count,), jnp.int32)

    packed = pl.pallas_call(
        functools.partial(pack_kernel, capacity, chunks, float(list_blk)),
        out_shape=jax.ShapeDtypeStruct(
            (tile_count, capacity * chunks + 1, atom_orb, LANES), jnp.bfloat16
        ),
        in_specs=[HBM_SPEC] * 3,
        out_specs=VMEM_SPEC,
        scratch_shapes=[
            pltpu.SMEM((slab_count,), jnp.int32),
            pltpu.SMEM((slab_count,), jnp.int32),
            pltpu.VMEM(dm_slabs.shape, dm_slabs.dtype),
            counts,
            pltpu.VMEM((tile_count, atom_orb, LANES), jnp.float32),
            pltpu.SemaphoreType.DMA((3,)),
        ],
        compiler_params=grant(4),
        name="pack",
    )(in_hbm(slab_tile), in_hbm(slab_place), in_hbm(dm_slabs))
    arrived = lax.all_to_all(packed, ("gx", "gy"), split_axis=0, concat_axis=0, tiled=True)
    half = plane // 2
    half_points = tile_points // 2
    piece = 4 * half
    bf16 = lambda *shape: jax.ShapeDtypeStruct(shape, jnp.bfloat16)
    f32 = lambda *shape: jax.ShapeDtypeStruct(shape, jnp.float32)
    near, far = pl.pallas_call(
        functools.partial(turn_kernel, size_x),
        out_shape=(
            pltpu.VMEM((list_orb, half_points), jnp.bfloat16),
            bf16(list_orb, half_points),
        ),
        in_specs=[HBM_SPEC],
        out_specs=(VMEM_SPEC, HBM_SPEC),
        scratch_shapes=[
            pltpu.VMEM((tile_points, list_orb), jnp.bfloat16),
            pltpu.VMEM((list_orb, half_points), jnp.bfloat16),
            pltpu.SemaphoreType.DMA((size_x // 2,)),
            pltpu.SemaphoreType.DMA((1,)),
        ],
        compiler_params=grant(20),
        cost_estimate=cost(0, 4 * tile_points * list_orb),
        name="turn",
    )(in_hbm(orbital_values.reshape(tile_points, list_orb)))

    slots = LANES * ((tile_count * capacity + LANES - 1) // LANES)
    product = 2 * half_points * list_orb * list_orb
    near_y, places, matrix, far = pl.pallas_call(
        functools.partial(near_kernel, capacity, chunks, piece),
        out_shape=(
            f32(size_x, half),
            jax.ShapeDtypeStruct((1, slots), jnp.int32),
            bf16(list_orb, list_orb),
            pltpu.VMEM((list_orb, half_points), jnp.bfloat16),
        ),
        in_specs=[VMEM_SPEC, VMEM_SPEC, HBM_SPEC],
        out_specs=(VMEM_SPEC,) * 4,
        scratch_shapes=[
            pltpu.VMEM((tile_count * capacity * atom_orb, LANES), jnp.float32),
            pltpu.SemaphoreType.DMA((1,)),
        ],
        compiler_params=grant(20),
        cost_estimate=cost(product, 2 * half_points * list_orb),
        name="near",
    )(arrived, near, in_hbm(far))
    rows = lax.axis_size("gy")
    pair = [(i, i ^ 1) for i in range(rows)]
    wrap = [(i, (i - 1 + 2 * (i % 2)) % rows) for i in range(rows)]
    from_wrap = lax.ppermute(near_y, "gy", wrap)
    far_y = pl.pallas_call(
        functools.partial(far_kernel, piece),
        out_shape=f32(size_x, half),
        in_specs=[VMEM_SPEC, VMEM_SPEC],
        out_specs=VMEM_SPEC,
        compiler_params=grant(20),
        cost_estimate=cost(product, 2 * half_points * list_orb),
        name="far",
    )(matrix, far)
    from_pair = lax.ppermute(far_y, "gy", pair)

    wide = 2 * plane
    own, top, bottom = pl.pallas_call(
        join_kernel,
        out_shape=(f32(size_x, wide), f32(RADIUS, wide), f32(RADIUS, wide)),
        in_specs=[VMEM_SPEC] * 4,
        out_specs=(VMEM_SPEC,) * 3,
        compiler_params=grant(2),
        name="join",
    )(near_y, far_y, from_wrap, from_pair)
    layers = lax.axis_size("gz")
    blocks = []
    for shift in {1: [0], 2: [0, 1]}.get(layers, [0, 1, -1]):
        blocks.append(moved(bottom, {"gx": 1, "gz": shift}))
        blocks.append(moved(own, {"gz": shift}) if shift else own)
        blocks.append(moved(top, {"gx": -1, "gz": shift}))
    parts = len(blocks) // 3
    tables = band_tables(size_z, parts - 1)
    lanes = tables[0].shape[1]
    wide_x, wide_y = size_x + 2 * RADIUS, size_y + 2 * RADIUS
    potential, field = pl.pallas_call(
        functools.partial(filter_kernel, parts),
        out_shape=(pltpu.VMEM((size_x, size_y, size_z), jnp.float32), f32(size_x, plane)),
        in_specs=[VMEM_SPEC] * (len(tables) + len(blocks)),
        out_specs=(VMEM_SPEC,) * 2,
        scratch_shapes=[
            pltpu.VMEM((wide_y, wide_x, parts * size_z), jnp.float32),
            pltpu.VMEM((wide_y, wide_x, lanes), jnp.float32),
            pltpu.VMEM((size_y, wide_x, lanes), jnp.float32),
            pltpu.VMEM((size_y, size_x, lanes), jnp.float32),
        ],
        compiler_params=grant(12),
        name="filter",
    )(*map(jnp.asarray, tables), *blocks)

    returned = pl.pallas_call(
        functools.partial(
            potential_kernel, capacity, chunks, atom_orb, float(tile_points) ** (-0.5), 2 * piece
        ),
        out_shape=bf16(tile_count, capacity, atom_orb, list_orb),
        in_specs=[VMEM_SPEC] * 4,
        out_specs=VMEM_SPEC,
        scratch_shapes=[
            pltpu.VMEM((list_orb, list_orb), jnp.float32),
            pltpu.SMEM((1, slots), jnp.int32),
            pltpu.SemaphoreType.DMA((1,)),
        ],
        compiler_params=grant(20),
        name="potential",
    )(places, field, near, far)
    back = lax.all_to_all(returned, ("gx", "gy"), split_axis=0, concat_axis=0, tiled=True)
    potential = pl.pallas_call(
        write_kernel,
        out_shape=f32(size_x, size_y, size_z),
        in_specs=[VMEM_SPEC],
        out_specs=HBM_SPEC,
        scratch_shapes=[pltpu.SemaphoreType.DMA((1,))],
        compiler_params=grant(2),
        name="write",
    )(potential)
    own_rows = pl.pallas_call(
        functools.partial(unpack_kernel, tile_count),
        out_shape=bf16(slab_count, atom_orb, list_orb),
        in_specs=[SMEM_SPEC, VMEM_SPEC],
        out_specs=HBM_SPEC,
        scratch_shapes=[counts, pltpu.SemaphoreType.DMA((1,))],
        compiler_params=grant(4),
        name="unpack",
    )(slab_tile, back)
    return (potential, own_rows)


def solution(mesh):
    placed = (
        P("gx", "gy", "gz", None),
        P(("gx", "gy", "gz"), None, None),
        P(("gx", "gy", "gz")),
        P(("gx", "gy", "gz")),
    )

    return jax.shard_map(
        local,
        mesh=mesh,
        in_specs=placed,
        out_specs=(P("gx", "gy", "gz"), P(("gx", "gy", "gz"), None, None)),
        check_vma=False,
    )
```

profile of v0, /device:TPU:0, one launch (start us, length us, event | category | flops | bytes accessed | tf_op | source)
XLA Modules:
  0.0 72.5 jit_solution(5320264671244673651)
XLA Ops:
  0.6 2.1 %pack.1 = bf16[16,19,8,128]{3,2,1,0:T(8,128)(2,1)} custom-call(s32[48]{0:T(128)} %tile_ref.1, s32[48]{0:T(128)} %place_hbm.1, bf16[48,8,384]{2,1,0:T(8,128)(2,1)} %slab_hbm.1), custom_call_target="tpu_custom_call" | custom-call | tf_op jit(solution)/shard_map/pack/pallas_call | solution.py:358
  2.8 7.4 %all-to-all-start = ((bf16[16,19,8,128]{3,2,1,0:T(8,128)(2,1)}), bf16[16,19,8,128]{3,2,1,0:T(8,128)(2,1)S(1)}, u32[]{:S(2)}, u32[]{:S(2)}) async-start(bf16[16,19,8,128]{3,2,1,0:T(8,128)(2,1)} %pack.1), calls=%async_computation | async-start | bytes 1245184 | tf_op jit(solution)/shard_map/all_to_all | solution.py:376
  10.2 3.1 %turn.1 = (bf16[384,3072]{1,0:T(8,128)(2,1)S(1)}, bf16[384,3072]{1,0:T(8,128)(2,1)S(1)}) custom-call(bf16[6144,384]{1,0:T(8,128)(2,1)} %bitcast.1), custom_call_target="tpu_custom_call" | custom-call | bytes 9437184 | tf_op jit(solution)/shard_map/turn/pallas_call | solution.py:382
  13.3 0.0 copy-start
  13.3 1.4 %copy-done = bf16[384,3072]{1,0:T(8,128)(2,1)} copy-done((bf16[384,3072]{1,0:T(8,128)(2,1)}, bf16[384,3072]{1,0:T(8,128)(2,1)S(1)}, u32[]{:S(2)}) %copy-start) | copy-done | bytes 2359320
  14.7 13.2 %all-to-all-done.arrived_ref = bf16[16,19,8,128]{3,2,1,0:T(8,128)(2,1)S(1)} async-done(((bf16[16,19,8,128]{3,2,1,0:T(8,128)(2,1)}), bf16[16,19,8,128]{3,2,1,0:T(8,128)(2,1)S(1)}, u32[]{:S(2)}, u32[]{:S(2)}) %all-to-all-start) | async-done | bytes 622624 | tf_op jit(solution)/shard_map/all_to_all | solution.py:376
  27.9 2.0 %near.1 = (f32[16,192]{1,0:T(8,128)S(1)}, s32[1,128]{1,0:T(1,128)S(1)}, bf16[384,384]{1,0:T(8,128)(2,1)S(1)}, bf16[384,3072]{1,0:T(8,128)(2,1)S(1)}) custom-call(bf16[16,19,8,128]{3,2,1,0:T(8,128)(2,1)S(1)} %all-to-all-done.arrived_ref, bf16[384,3072]{1,0:T(8,128)(2,1)S(1)} %get-tuple-element.13.near_ref, bf16[384,3072]{1,0:T(8,128)(2,1)} %copy-done), custom_call_target="tpu_custom_call" | custom-call | flops 905969664 | bytes 2359296 | tf_op jit(solution)/shard_map/near/pallas_call | solution.py:403
  29.8 0.0 copy-start.1
  29.9 0.0 copy-start.2
  29.9 0.0 copy-start.3
  29.9 0.0 copy-start.4
  29.9 0.0 copy-start.5
  29.9 1.5 %far.1.far_ref = f32[16,192]{1,0:T(8,128)S(1)} custom-call(bf16[384,384]{1,0:T(8,128)(2,1)S(1)} %get-tuple-element.16.turned_ref, bf16[384,3072]{1,0:T(8,128)(2,1)S(1)} %get-tuple-element.17.far_ref), custom_call_target="tpu_custom_call" | custom-call | flops 905969664 | bytes 2359296 | tf_op jit(solution)/shard_map/far/pallas_call | solution.py:425
  31.4 0.0 collective-permute-start.1
  31.4 1.1 %collective-permute-start = (f32[16,192]{1,0:T(8,128)S(1)}, f32[16,192]{1,0:T(8,128)S(1)}, u32[]{:S(2)}, u32[]{:S(2)}) collective-permute-start(f32[16,192]{1,0:T(8,128)S(1)} %get-tuple-element.15.near_ref), channel_id=1, source_target_pairs={{0,6},{2,4},{4,2},{6,0},{1,7},{3,5},{5,3},{7,1},{8,14},{10,12},{12... | collective-permute-start | bytes 36872 | tf_op jit(solution)/shard_map/ppermute | solution.py:424
  32.5 2.6 %collective-permute-done.1.pair_ref = f32[16,192]{1,0:T(8,128)S(1)} collective-permute-done((f32[16,192]{1,0:T(8,128)S(1)}, f32[16,192]{1,0:T(8,128)S(1)}, u32[]{:S(2)}, u32[]{:S(2)}) %collective-permute-start.1) | collective-permute-done | bytes 12320 | tf_op jit(solution)/shard_map/ppermute | solution.py:434
  35.2 1.9 %collective-permute-done.wrap_ref = f32[16,192]{1,0:T(8,128)S(1)} collective-permute-done((f32[16,192]{1,0:T(8,128)S(1)}, f32[16,192]{1,0:T(8,128)S(1)}, u32[]{:S(2)}, u32[]{:S(2)}) %collective-permute-start) | collective-permute-done | bytes 12320 | tf_op jit(solution)/shard_map/ppermute | solution.py:424
  37.1 0.1 join.1
  37.1 1.5 %collective-permute-start.5 = (f32[16,768]{1,0:T(8,128)S(1)}, f32[16,768]{1,0:T(8,128)S(1)}, u32[]{:S(2)}, u32[]{:S(2)}) collective-permute-start(f32[16,768]{1,0:T(8,128)S(1)} %get-tuple-element.19.refs_6_), channel_id=1, source_target_pairs={{0,1},{1,0},{2,3},{3,2},{4,5},{5,4},{6,7},{7,6},{8,9},{9,8},{10,11... | collective-permute-start | bytes 147464 | tf_op jit(solution)/shard_map/ppermute | solution.py:316
  38.7 0.0 collective-permute-start.4
  38.7 1.3 %collective-permute-start.2 = (f32[8,768]{1,0:T(8,128)S(1)}, f32[8,768]{1,0:T(8,128)S(1)}, u32[]{:S(2)}, u32[]{:S(2)}) collective-permute-start(f32[8,768]{1,0:T(8,128)S(1)} %get-tuple-element.18), channel_id=1, source_target_pairs={{0,8},{1,9},{8,16},{9,17},{16,24},{17,25},{24,0},{25,1},{2,10},{3,... | collective-permute-start | bytes 73736 | tf_op jit(solution)/shard_map/ppermute | solution.py:316
  40.0 1.4 %collective-permute-start.6 = (f32[8,768]{1,0:T(8,128)S(1)}, f32[8,768]{1,0:T(8,128)S(1)}, u32[]{:S(2)}, u32[]{:S(2)}) collective-permute-start(f32[8,768]{1,0:T(8,128)S(1)} %get-tuple-element.20), channel_id=1, source_target_pairs={{0,25},{1,24},{8,1},{9,0},{16,9},{17,8},{24,17},{25,16},{2,27},{3,... | collective-permute-start | bytes 73736 | tf_op jit(solution)/shard_map/ppermute | solution.py:316
  41.3 0.7 collective-permute-start.3
  42.0 0.8 %collective-permute-done.4.refs_8_ = f32[8,768]{1,0:T(8,128)S(1)} collective-permute-done((f32[8,768]{1,0:T(8,128)S(1)}, f32[8,768]{1,0:T(8,128)S(1)}, u32[]{:S(2)}, u32[]{:S(2)}) %collective-permute-start.4) | collective-permute-done | bytes 24608 | tf_op jit(solution)/shard_map/ppermute | solution.py:316
  42.8 0.0 collective-permute-done.2.refs_5_
  42.8 0.4 collective-permute-done.6.refs_10_
  43.2 0.3 collective-permute-done.3.refs_7_
  43.5 0.0 collective-permute-done.5.refs_9_
  43.5 0.0 copy-done.1
  43.5 0.0 copy-done.2
  43.5 0.0 copy-done.3
  43.5 0.0 copy-done.4
  43.5 0.0 copy-done.5
  43.6 2.2 %filter.1 = (f32[16,16,24]{2,1,0:T(8,128)S(1)}, f32[16,384]{1,0:T(8,128)S(1)}) custom-call(f32[16,192]{1,0:T(8,128)S(1)} %copy-done.5, bf16[48,192]{1,0:T(8,128)(2,1)S(1)} %copy-done.4, bf16[48,192]{1,0:T(8,128)(2,1)S(1)} %copy-done.3, bf16[192,24]{1,0:T(8,128)(2,1)S(1)} %copy-done.2, bf16[192,24]{1,0:T(8,128)(2,1)S(1)} %copy-done.1, ...), custom_call_target="tpu_custom_call" | custom-call | tf_op jit(solution)/shard_map/filter/pallas_call | solution.py:455
  45.8 0.0 copy-start.6
  45.8 4.6 %potential.1 = bf16[16,6,8,384]{3,2,1,0:T(8,128)(2,1)} custom-call(s32[1,128]{1,0:T(1,128)S(1)} %get-tuple-element.22.place_vmem, f32[16,384]{1,0:T(8,128)S(1)} %get-tuple-element.23.field_ref, bf16[384,3072]{1,0:T(8,128)(2,1)S(1)} %get-tuple-element.13.near_ref, bf16[384,3072]{1,0:T(8,128)(2,1)S(1)} %get-tuple-element.17.far_ref), custom_call_target="tpu_custom_call" | custom-call | tf_op jit(solution)/shard_map/potential/pallas_call | solution.py:470
  50.4 3.8 %all-to-all-start.1 = ((bf16[16,6,8,384]{3,2,1,0:T(8,128)(2,1)}), bf16[16,6,8,384]{3,2,1,0:T(8,128)(2,1)S(1)}, u32[]{:S(2)}, u32[]{:S(2)}) async-start(bf16[16,6,8,384]{3,2,1,0:T(8,128)(2,1)} %potential.1), calls=%async_computation.1 | async-start | bytes 1179648 | tf_op jit(solution)/shard_map/all_to_all | solution.py:485
  54.1 0.7 write.1
  54.8 16.3 %all-to-all-done.1.back_ref = bf16[16,6,8,384]{3,2,1,0:T(8,128)(2,1)S(1)} async-done(((bf16[16,6,8,384]{3,2,1,0:T(8,128)(2,1)}), bf16[16,6,8,384]{3,2,1,0:T(8,128)(2,1)S(1)}, u32[]{:S(2)}, u32[]{:S(2)}) %all-to-all-start.1) | async-done | bytes 589856 | tf_op jit(solution)/shard_map/all_to_all | solution.py:485
  71.1 0.0 copy-done.6
  71.1 1.4 %unpack.1 = bf16[48,8,384]{2,1,0:T(8,128)(2,1)} custom-call(s32[48]{0:T(128)S(1)} %copy-done.6, bf16[16,6,8,384]{3,2,1,0:T(8,128)(2,1)S(1)} %all-to-all-done.1.back_ref), custom_call_target="tpu_custom_call" | custom-call | tf_op jit(solution)/shard_map/unpack/pallas_call | solution.py:495
Async XLA Ops:
  2.8 25.1 %all-to-all-start = ((bf16[16,19,8,128]{3,2,1,0:T(8,128)(2,1)}), bf16[16,19,8,128]{3,2,1,0:T(8,128)(2,1)S(1)}, u32[]{:S(2)}, u32[]{:S(2)}) async-start(bf16[16,19,8,128]{3,2,1,0:T(8,128)(2,1)} %pack.1), calls=%async_computation | async-start | bytes 1245184 | tf_op jit(solution)/shard_map/all_to_all | solution.py:376
  13.3 1.4 %copy-start = (bf16[384,3072]{1,0:T(8,128)(2,1)}, bf16[384,3072]{1,0:T(8,128)(2,1)S(1)}, u32[]{:S(2)}) copy-start(bf16[384,3072]{1,0:T(8,128)(2,1)S(1)} %get-tuple-element.14.far_hbm) | copy-start | bytes 7077892
  29.8 13.7 %copy-start.1 = (bf16[192,24]{1,0:T(8,128)(2,1)S(1)}, bf16[192,24]{1,0:T(8,128)(2,1)}, u32[]{:S(2)}) copy-start(bf16[192,24]{1,0:T(8,128)(2,1)} %constant.14.clone.refs_4_) | copy-start | bytes 27652
  29.9 13.7 %copy-start.2 = (bf16[192,24]{1,0:T(8,128)(2,1)S(1)}, bf16[192,24]{1,0:T(8,128)(2,1)}, u32[]{:S(2)}) copy-start(bf16[192,24]{1,0:T(8,128)(2,1)} %constant.13.clone.refs_3_) | copy-start | bytes 27652
  29.9 13.7 %copy-start.3 = (bf16[48,192]{1,0:T(8,128)(2,1)S(1)}, bf16[48,192]{1,0:T(8,128)(2,1)}, u32[]{:S(2)}) copy-start(bf16[48,192]{1,0:T(8,128)(2,1)} %constant.12.clone.refs_2_) | copy-start | bytes 55300
  29.9 13.7 %copy-start.4 = (bf16[48,192]{1,0:T(8,128)(2,1)S(1)}, bf16[48,192]{1,0:T(8,128)(2,1)}, u32[]{:S(2)}) copy-start(bf16[48,192]{1,0:T(8,128)(2,1)} %constant.11.clone.refs_1_) | copy-start | bytes 55300
  29.9 13.7 %copy-start.5 = (f32[16,192]{1,0:T(8,128)S(1)}, f32[16,192]{1,0:T(8,128)}, u32[]{:S(2)}) copy-start(f32[16,192]{1,0:T(8,128)} %constant.10.clone.refs_0_) | copy-start | bytes 36868
  31.4 3.7 %collective-permute-start.1 = (f32[16,192]{1,0:T(8,128)S(1)}, f32[16,192]{1,0:T(8,128)S(1)}, u32[]{:S(2)}, u32[]{:S(2)}) collective-permute-start(f32[16,192]{1,0:T(8,128)S(1)} %far.1.far_ref), channel_id=1, source_target_pairs={{0,2},{2,0},{4,6},{6,4},{1,3},{3,1},{5,7},{7,5},{8,10},{10,8},{12,... | collective-permute-start | bytes 36872 | tf_op jit(solution)/shard_map/ppermute | solution.py:434
  31.4 5.6 %collective-permute-start = (f32[16,192]{1,0:T(8,128)S(1)}, f32[16,192]{1,0:T(8,128)S(1)}, u32[]{:S(2)}, u32[]{:S(2)}) collective-permute-start(f32[16,192]{1,0:T(8,128)S(1)} %get-tuple-element.15.near_ref), channel_id=1, source_target_pairs={{0,6},{2,4},{4,2},{6,0},{1,7},{3,5},{5,3},{7,1},{8,14},{10,12},{12... | collective-permute-start | bytes 36872 | tf_op jit(solution)/shard_map/ppermute | solution.py:424
  37.1 6.4 %collective-permute-start.5 = (f32[16,768]{1,0:T(8,128)S(1)}, f32[16,768]{1,0:T(8,128)S(1)}, u32[]{:S(2)}, u32[]{:S(2)}) collective-permute-start(f32[16,768]{1,0:T(8,128)S(1)} %get-tuple-element.19.refs_6_), channel_id=1, source_target_pairs={{0,1},{1,0},{2,3},{3,2},{4,5},{5,4},{6,7},{7,6},{8,9},{9,8},{10,11... | collective-permute-start | bytes 147464 | tf_op jit(solution)/shard_map/ppermute | solution.py:316
  38.7 4.2 %collective-permute-start.4 = (f32[8,768]{1,0:T(8,128)S(1)}, f32[8,768]{1,0:T(8,128)S(1)}, u32[]{:S(2)}, u32[]{:S(2)}) collective-permute-start(f32[8,768]{1,0:T(8,128)S(1)} %get-tuple-element.18), channel_id=1, source_target_pairs={{0,9},{1,8},{8,17},{9,16},{16,25},{17,24},{24,1},{25,0},{2,11},{3,... | collective-permute-start | bytes 73736 | tf_op jit(solution)/shard_map/ppermute | solution.py:316
  38.7 4.2 %collective-permute-start.2 = (f32[8,768]{1,0:T(8,128)S(1)}, f32[8,768]{1,0:T(8,128)S(1)}, u32[]{:S(2)}, u32[]{:S(2)}) collective-permute-start(f32[8,768]{1,0:T(8,128)S(1)} %get-tuple-element.18), channel_id=1, source_target_pairs={{0,8},{1,9},{8,16},{9,17},{16,24},{17,25},{24,0},{25,1},{2,10},{3,... | collective-permute-start | bytes 73736 | tf_op jit(solution)/shard_map/ppermute | solution.py:316
  40.0 3.3 %collective-permute-start.6 = (f32[8,768]{1,0:T(8,128)S(1)}, f32[8,768]{1,0:T(8,128)S(1)}, u32[]{:S(2)}, u32[]{:S(2)}) collective-permute-start(f32[8,768]{1,0:T(8,128)S(1)} %get-tuple-element.20), channel_id=1, source_target_pairs={{0,25},{1,24},{8,1},{9,0},{16,9},{17,8},{24,17},{25,16},{2,27},{3,... | collective-permute-start | bytes 73736 | tf_op jit(solution)/shard_map/ppermute | solution.py:316
  41.3 2.2 %collective-permute-start.3 = (f32[8,768]{1,0:T(8,128)S(1)}, f32[8,768]{1,0:T(8,128)S(1)}, u32[]{:S(2)}, u32[]{:S(2)}) collective-permute-start(f32[8,768]{1,0:T(8,128)S(1)} %get-tuple-element.20), channel_id=1, source_target_pairs={{0,24},{1,25},{8,0},{9,1},{16,8},{17,9},{24,16},{25,17},{2,26},{3,... | collective-permute-start | bytes 73736 | tf_op jit(solution)/shard_map/ppermute | solution.py:316
  45.8 25.3 %copy-start.6 = (s32[48]{0:T(128)S(1)}, s32[48]{0:T(128)}, u32[]{:S(2)}) copy-start(s32[48]{0:T(128)} %tile_ref.1) | copy-start | bytes 580
  50.4 20.7 %all-to-all-start.1 = ((bf16[16,6,8,384]{3,2,1,0:T(8,128)(2,1)}), bf16[16,6,8,384]{3,2,1,0:T(8,128)(2,1)S(1)}, u32[]{:S(2)}, u32[]{:S(2)}) async-start(bf16[16,6,8,384]{3,2,1,0:T(8,128)(2,1)} %potential.1), calls=%async_computation.1 | async-start | bytes 1179648 | tf_op jit(solution)/shard_map/all_to_all | solution.py:485
where the time goes:
time: 72.9 us; the launch traced here: 72.5 us
  waiting for transfers between devices  35.5 us (49%)
  Pallas kernels  17.7 us (24%)
  starting transfers between devices  17.1 us (23%)
  local copies, waits for them, and re-layouts  1.47 us (2%)
  between operations  0.78 us (1%)
    all_to_all x1, waiting for transfers between devices, local(): lax.all_to_all(returned, ('gx', 'gy'), split_axis=0, concat_axis=0, tiled...  16.3 us
    all_to_all x1, waiting for transfers between devices, local(): lax.all_to_all(packed, ('gx', 'gy'), split_axis=0, concat_axis=0, tiled=T...  13.2 us
    all_to_all x1, starting transfers between devices, local(): lax.all_to_all(packed, ('gx', 'gy'), split_axis=0, concat_axis=0, tiled=T...  7.42 us
    ppermute x5, starting transfers between devices, moved(): return lax.ppermute(block, axes, pairs)  4.86 us
    pallas_call x1, Pallas kernels, local(): pl.pallas_call(functools.partial(potential_kernel, capacity, chunks, atom...  4.55 us
    all_to_all x1, starting transfers between devices, local(): lax.all_to_all(returned, ('gx', 'gy'), split_axis=0, concat_axis=0, tiled...  3.75 us
    pallas_call x1, Pallas kernels, local(): pl.pallas_call(functools.partial(turn_kernel, size_x), out_shape=(pltpu.V...  3.07 us
    ppermute x1, waiting for transfers between devices, local(): from_pair = lax.ppermute(far_y, 'gy', pair)  2.64 us
  transfers between devices with their start and end apart: 9, of which 7 were waited for; matrix products, arithmetic and copies ran while one was open for 0% of the time, Pallas kernels for 5%

commit v1 on v0

--- a/solution.py
+++ b/solution.py
@@ -246,16 +246,21 @@
 
 
 def potential_kernel(
-    capacity, chunks, rows, weight, piece, place_vmem, field_ref, near_ref, far_ref,
-    out_ref, total_ref, place_ref, sem,
+    capacity, weight, piece, place_vmem, grid_ref, field_ref, near_ref, far_ref,
+    out_ref, grid_hbm, right_ref, corner_ref, whole_ref, place_ref, sems,
 ):
-    copy = pltpu.make_async_copy(place_vmem, place_ref, sem.at[0])
-    copy.start()
-    list_orb, points = near_ref.shape
+    copies = [
+        pltpu.make_async_copy(place_vmem, place_ref, sems.at[0]),
+        pltpu.make_async_copy(grid_ref, grid_hbm, sems.at[1]),
+    ]
+    for copy in copies:
+        copy.start()
+    points = near_ref.shape[1]
     half = field_ref.shape[1] // 2
     odd = odd_row() == 1
     low, high = field_ref[:, :half] * weight, field_ref[:, half:] * weight
     first = True
+    over_points = (((1,), (1,)), ((), ()))
     for values_ref, source in (
         (near_ref, jnp.where(odd, high, low)),
         (far_ref, jnp.where(odd, low, high)),
@@ -270,30 +275,32 @@
             )
             block = values_ref[:, q * piece : (q + 1) * piece]
             weighted = (field * block.astype(jnp.float32)).astype(jnp.bfloat16)
-            term = lax.dot_general(
-                block, weighted, (((1,), (1,)), ((), ())), preferred_element_type=jnp.float32
+            right = lax.dot_general(
+                block, weighted[LANES:], over_points, preferred_element_type=jnp.float32
             )
-            total_ref[...] = term if first else total_ref[...] + term
+            corner = lax.dot_general(
+                block[:LANES], weighted[:LANES], over_points, preferred_element_type=jnp.float32
+            )
+            right_ref[...] = right if first else right_ref[...] + right
+            corner_ref[...] = corner if first else corner_ref[...] + corner
             first = False
 
-    copy.wait()
-    last = list_orb // rows - 1
+    blocks, rows, _ = whole_ref.shape
+    edge = LANES // rows
+    whole_ref[:edge, :, :LANES] = corner_ref[...].reshape(edge, rows, -1).astype(jnp.bfloat16)
+    whole_ref[edge:, :, :LANES] = (
+        right_ref[:LANES].T.reshape(blocks - edge, rows, -1).astype(jnp.bfloat16)
+    )
+    whole_ref[:, :, LANES:] = right_ref[...].reshape(blocks, rows, -1).astype(jnp.bfloat16)
+    for copy in copies:
+        copy.wait()
 
     def visit(j, carry):
         t, k = j // capacity, j % capacity
-        row = pl.multiple_of(jnp.minimum(place_ref[0, j], last) * rows, rows)
-        for c in range(chunks):
-            lanes = slice(c * LANES, (c + 1) * LANES)
-            out_ref[t, k, :, lanes] = total_ref[pl.ds(row, rows), lanes].astype(jnp.bfloat16)
+        out_ref[t, k] = whole_ref[jnp.minimum(place_ref[0, j], blocks - 1)]
         return carry
 
-    lax.fori_loop(0, out_ref.shape[0] * capacity, visit, 0, unroll=4)
-
-
-def write_kernel(grid_ref, grid_hbm, sem):
-    copy = pltpu.make_async_copy(grid_ref, grid_hbm, sem.at[0])
-    copy.start()
-    copy.wait()
+    lax.fori_loop(0, out_ref.shape[0] * capacity, visit, 0, unroll=16)
 
 
 def unpack_kernel(tile_count, tile_ref, back_ref, out_hbm, count_ref, sem):
@@ -467,31 +474,27 @@
         name="filter",
     )(*map(jnp.asarray, tables), *blocks)
 
-    returned = pl.pallas_call(
+    returned, potential = pl.pallas_call(
         functools.partial(
-            potential_kernel, capacity, chunks, atom_orb, float(tile_points) ** (-0.5), 2 * piece
+            potential_kernel, capacity, float(tile_points) ** (-0.5), 2 * piece
         ),
-        out_shape=bf16(tile_count, capacity, atom_orb, list_orb),
-        in_specs=[VMEM_SPEC] * 4,
-        out_specs=VMEM_SPEC,
+        out_shape=(
+            bf16(tile_count, capacity, atom_orb, list_orb),
+            f32(size_x, size_y, size_z),
+        ),
+        in_specs=[VMEM_SPEC] * 5,
+        out_specs=(VMEM_SPEC, HBM_SPEC),
         scratch_shapes=[
-            pltpu.VMEM((list_orb, list_orb), jnp.float32),
+            pltpu.VMEM((list_orb, list_orb - LANES), jnp.float32),
+            pltpu.VMEM((LANES, LANES), jnp.float32),
+            pltpu.VMEM((list_blk, atom_orb, list_orb), jnp.bfloat16),
             pltpu.SMEM((1, slots), jnp.int32),
-            pltpu.SemaphoreType.DMA((1,)),
+            pltpu.SemaphoreType.DMA((2,)),
         ],
         compiler_params=grant(20),
         name="potential",
-    )(places, field, near, far)
+    )(places, potential, field, near, far)
     back = lax.all_to_all(returned, ("gx", "gy"), split_axis=0, concat_axis=0, tiled=True)
-    potential = pl.pallas_call(
-        write_kernel,
-        out_shape=f32(size_x, size_y, size_z),
-        in_specs=[VMEM_SPEC],
-        out_specs=HBM_SPEC,
-        scratch_shapes=[pltpu.SemaphoreType.DMA((1,))],
-        compiler_params=grant(2),
-        name="write",
-    )(potential)
     own_rows = pl.pallas_call(
         functools.partial(unpack_kernel, tile_count),
         out_shape=bf16(slab_count, atom_orb, list_orb),

time: 72.9 us -> 71.3 us (0.978)
  blocking collectives: 0 us -> 20.8 us
  waiting for transfers between devices: 35.5 us -> 19.2 us
  starting transfers between devices: 17.1 us -> 13.4 us
  Pallas kernels: 17.7 us -> 15.4 us
    all_to_all x0 -> x1, blocking collectives: none -> 20.8 us  [local(): lax.all_to_all(returned, ('gx', 'gy'), split_axis=0, concat_axis=0, tiled...]
    all_to_all x1 -> x0, waiting for transfers between devices: 16.3 us -> none  [local(): lax.all_to_all(returned, ('gx', 'gy'), split_axis=0, concat_axis=0, tiled...]
    all_to_all x1 -> x0, starting transfers between devices: 3.75 us -> none  [local(): lax.all_to_all(returned, ('gx', 'gy'), split_axis=0, concat_axis=0, tiled...]
    pallas_call x2 -> x1, Pallas kernels: 5.22 us -> 2.93 us  [local(): pl.pallas_call(functools.partial(potential_kernel, capacity, float(tile_p...]
  transfers between devices with their start and end apart: 9 -> 8, of which waited for: 7 -> 6; matrix products, arithmetic and copies ran while one was open for 0% -> 0% of each run, Pallas kernels for 5% -> 4%
where the time goes in v1:
time: 71.3 us; the launch traced here: 71 us
  blocking collectives  20.8 us (29%)
  waiting for transfers between devices  19.2 us (27%)
  Pallas kernels  15.4 us (22%)
  starting transfers between devices  13.4 us (19%)
  local copies, waits for them, and re-layouts  1.45 us (2%)
  between operations  0.76 us (1%)
    all_to_all x1, blocking collectives, local(): lax.all_to_all(returned, ('gx', 'gy'), split_axis=0, concat_axis=0, tiled...  20.8 us
    all_to_all x1, waiting for transfers between devices, local(): lax.all_to_all(packed, ('gx', 'gy'), split_axis=0, concat_axis=0, tiled=T...  13.2 us
    all_to_all x1, starting transfers between devices, local(): lax.all_to_all(packed, ('gx', 'gy'), split_axis=0, concat_axis=0, tiled=T...  7.42 us
    ppermute x5, starting transfers between devices, moved(): return lax.ppermute(block, axes, pairs)  4.86 us
    pallas_call x1, Pallas kernels, local(): pl.pallas_call(functools.partial(turn_kernel, size_x), out_shape=(pltpu.V...  3.07 us
    pallas_call x1, Pallas kernels, local(): pl.pallas_call(functools.partial(potential_kernel, capacity, float(tile_p...  2.93 us
    ppermute x1, waiting for transfers between devices, local(): from_pair = lax.ppermute(far_y, 'gy', pair)  2.65 us
    pallas_call x1, Pallas kernels, local(): pl.pallas_call(functools.partial(filter_kernel, parts), out_shape=(pltpu....  2.25 us
  transfers between devices with their start and end apart: 8, of which 6 were waited for; matrix products, arithmetic and copies ran while one was open for 0% of the time, Pallas kernels for 4%

profile of v1, /device:TPU:0, one launch (start us, length us, event | category | flops | bytes accessed | tf_op | source)
XLA Modules:
  0.0 71.0 jit_solution(8719452379446611405)
XLA Ops:
  0.6 2.1 %pack.1 = bf16[16,19,8,128]{3,2,1,0:T(8,128)(2,1)} custom-call(s32[48]{0:T(128)} %tile_ref.1, s32[48]{0:T(128)} %place_hbm.1, bf16[48,8,384]{2,1,0:T(8,128)(2,1)} %slab_hbm.1), custom_call_target="tpu_custom_call" | custom-call | tf_op jit(solution)/shard_map/pack/pallas_call | solution.py:365
  2.8 7.4 %all-to-all-start = ((bf16[16,19,8,128]{3,2,1,0:T(8,128)(2,1)}), bf16[16,19,8,128]{3,2,1,0:T(8,128)(2,1)S(1)}, u32[]{:S(2)}, u32[]{:S(2)}) async-start(bf16[16,19,8,128]{3,2,1,0:T(8,128)(2,1)} %pack.1), calls=%async_computation | async-start | bytes 1245184 | tf_op jit(solution)/shard_map/all_to_all | solution.py:383
  10.2 3.1 %turn.1 = (bf16[384,3072]{1,0:T(8,128)(2,1)S(1)}, bf16[384,3072]{1,0:T(8,128)(2,1)S(1)}) custom-call(bf16[6144,384]{1,0:T(8,128)(2,1)} %bitcast.1), custom_call_target="tpu_custom_call" | custom-call | bytes 9437184 | tf_op jit(solution)/shard_map/turn/pallas_call | solution.py:389
  13.3 0.0 copy-start
  13.3 1.4 %copy-done = bf16[384,3072]{1,0:T(8,128)(2,1)} copy-done((bf16[384,3072]{1,0:T(8,128)(2,1)}, bf16[384,3072]{1,0:T(8,128)(2,1)S(1)}, u32[]{:S(2)}) %copy-start) | copy-done | bytes 2359320
  14.7 13.2 %all-to-all-done.arrived_ref = bf16[16,19,8,128]{3,2,1,0:T(8,128)(2,1)S(1)} async-done(((bf16[16,19,8,128]{3,2,1,0:T(8,128)(2,1)}), bf16[16,19,8,128]{3,2,1,0:T(8,128)(2,1)S(1)}, u32[]{:S(2)}, u32[]{:S(2)}) %all-to-all-start) | async-done | bytes 622624 | tf_op jit(solution)/shard_map/all_to_all | solution.py:383
  27.9 2.0 %near.1 = (f32[16,192]{1,0:T(8,128)S(1)}, s32[1,128]{1,0:T(1,128)S(1)}, bf16[384,384]{1,0:T(8,128)(2,1)S(1)}, bf16[384,3072]{1,0:T(8,128)(2,1)S(1)}) custom-call(bf16[16,19,8,128]{3,2,1,0:T(8,128)(2,1)S(1)} %all-to-all-done.arrived_ref, bf16[384,3072]{1,0:T(8,128)(2,1)S(1)} %get-tuple-element.15.near_ref, bf16[384,3072]{1,0:T(8,128)(2,1)} %copy-done), custom_call_target="tpu_custom_call" | custom-call | flops 905969664 | bytes 2359296 | tf_op jit(solution)/shard_map/near/pallas_call | solution.py:410
  29.8 0.0 copy-start.1
  29.9 0.0 copy-start.2
  29.9 0.0 copy-start.3
  29.9 0.0 copy-start.4
  29.9 0.0 copy-start.5
  29.9 1.5 %far.1.far_ref = f32[16,192]{1,0:T(8,128)S(1)} custom-call(bf16[384,384]{1,0:T(8,128)(2,1)S(1)} %get-tuple-element.19.turned_ref, bf16[384,3072]{1,0:T(8,128)(2,1)S(1)} %get-tuple-element.20.far_ref), custom_call_target="tpu_custom_call" | custom-call | flops 905969664 | bytes 2359296 | tf_op jit(solution)/shard_map/far/pallas_call | solution.py:432
  31.4 0.0 collective-permute-start.1
  31.5 1.1 %collective-permute-start = (f32[16,192]{1,0:T(8,128)S(1)}, f32[16,192]{1,0:T(8,128)S(1)}, u32[]{:S(2)}, u32[]{:S(2)}) collective-permute-start(f32[16,192]{1,0:T(8,128)S(1)} %get-tuple-element.18.near_ref), channel_id=1, source_target_pairs={{0,6},{2,4},{4,2},{6,0},{1,7},{3,5},{5,3},{7,1},{8,14},{10,12},{12... | collective-permute-start | bytes 36872 | tf_op jit(solution)/shard_map/ppermute | solution.py:431
  32.5 2.6 %collective-permute-done.1.pair_ref = f32[16,192]{1,0:T(8,128)S(1)} collective-permute-done((f32[16,192]{1,0:T(8,128)S(1)}, f32[16,192]{1,0:T(8,128)S(1)}, u32[]{:S(2)}, u32[]{:S(2)}) %collective-permute-start.1) | collective-permute-done | bytes 12320 | tf_op jit(solution)/shard_map/ppermute | solution.py:441
  35.2 1.9 %collective-permute-done.wrap_ref = f32[16,192]{1,0:T(8,128)S(1)} collective-permute-done((f32[16,192]{1,0:T(8,128)S(1)}, f32[16,192]{1,0:T(8,128)S(1)}, u32[]{:S(2)}, u32[]{:S(2)}) %collective-permute-start) | collective-permute-done | bytes 12320 | tf_op jit(solution)/shard_map/ppermute | solution.py:431
  37.1 0.1 join.1
  37.1 1.5 %collective-permute-start.5 = (f32[16,768]{1,0:T(8,128)S(1)}, f32[16,768]{1,0:T(8,128)S(1)}, u32[]{:S(2)}, u32[]{:S(2)}) collective-permute-start(f32[16,768]{1,0:T(8,128)S(1)} %get-tuple-element.22.refs_6_), channel_id=1, source_target_pairs={{0,1},{1,0},{2,3},{3,2},{4,5},{5,4},{6,7},{7,6},{8,9},{9,8},{10,11... | collective-permute-start | bytes 147464 | tf_op jit(solution)/shard_map/ppermute | solution.py:323
  38.7 0.0 collective-permute-start.4
  38.7 1.3 %collective-permute-start.2 = (f32[8,768]{1,0:T(8,128)S(1)}, f32[8,768]{1,0:T(8,128)S(1)}, u32[]{:S(2)}, u32[]{:S(2)}) collective-permute-start(f32[8,768]{1,0:T(8,128)S(1)} %get-tuple-element.21), channel_id=1, source_target_pairs={{0,8},{1,9},{8,16},{9,17},{16,24},{17,25},{24,0},{25,1},{2,10},{3,... | collective-permute-start | bytes 73736 | tf_op jit(solution)/shard_map/ppermute | solution.py:323
  40.0 1.4 %collective-permute-start.6 = (f32[8,768]{1,0:T(8,128)S(1)}, f32[8,768]{1,0:T(8,128)S(1)}, u32[]{:S(2)}, u32[]{:S(2)}) collective-permute-start(f32[8,768]{1,0:T(8,128)S(1)} %get-tuple-element.23), channel_id=1, source_target_pairs={{0,25},{1,24},{8,1},{9,0},{16,9},{17,8},{24,17},{25,16},{2,27},{3,... | collective-permute-start | bytes 73736 | tf_op jit(solution)/shard_map/ppermute | solution.py:323
  41.3 0.7 collective-permute-start.3
  42.0 0.8 %collective-permute-done.4.refs_8_ = f32[8,768]{1,0:T(8,128)S(1)} collective-permute-done((f32[8,768]{1,0:T(8,128)S(1)}, f32[8,768]{1,0:T(8,128)S(1)}, u32[]{:S(2)}, u32[]{:S(2)}) %collective-permute-start.4) | collective-permute-done | bytes 24608 | tf_op jit(solution)/shard_map/ppermute | solution.py:323
  42.8 0.0 collective-permute-done.2.refs_5_
  42.8 0.4 collective-permute-done.6.refs_10_
  43.2 0.3 collective-permute-done.3.refs_7_
  43.5 0.0 collective-permute-done.5.refs_9_
  43.5 0.0 copy-done.1
  43.5 0.0 copy-done.2
  43.5 0.0 copy-done.3
  43.5 0.0 copy-done.4
  43.6 0.0 copy-done.5
  43.6 2.2 %filter.1 = (f32[16,16,24]{2,1,0:T(8,128)S(1)}, f32[16,384]{1,0:T(8,128)S(1)}) custom-call(f32[16,192]{1,0:T(8,128)S(1)} %copy-done.5, bf16[48,192]{1,0:T(8,128)(2,1)S(1)} %copy-done.4, bf16[48,192]{1,0:T(8,128)(2,1)S(1)} %copy-done.3, bf16[192,24]{1,0:T(8,128)(2,1)S(1)} %copy-done.2, bf16[192,24]{1,0:T(8,128)(2,1)S(1)} %copy-done.1, ...), custom_call_target="tpu_custom_call" | custom-call | tf_op jit(solution)/shard_map/filter/pallas_call | solution.py:462
  45.8 0.0 copy-start.6
  45.8 2.9 %potential.1 = (bf16[16,6,8,384]{3,2,1,0:T(8,128)(2,1)S(1)}, f32[16,16,24]{2,1,0:T(8,128)}) custom-call(s32[1,128]{1,0:T(1,128)S(1)} %get-tuple-element.17.place_vmem, f32[16,16,24]{2,1,0:T(8,128)S(1)} %get-tuple-element.24.grid_ref, f32[16,384]{1,0:T(8,128)S(1)} %get-tuple-element.25.field_ref, bf16[384,3072]{1,0:T(8,128)(2,1)S(1)} %get-tuple-element.15.near_ref, ...), custom_call_target="tpu_custom_call" | custom-call | tf_op jit(solution)/shard_map/potential/pallas_call | solution.py:477
  48.8 20.8 %all_to_all.10.back_ref = bf16[16,6,8,384]{3,2,1,0:T(8,128)(2,1)S(1)} all-to-all(bf16[16,6,8,384]{3,2,1,0:T(8,128)(2,1)S(1)} %get-tuple-element.27), channel_id=1, replica_groups=mesh['gx'=4,'gy'=4,'gz'=2] {'gx','gy'}, dimensions={0} | all-to-all | bytes 1179648 | tf_op jit(solution)/shard_map/all_to_all | solution.py:497
  69.6 0.0 copy-done.6
  69.6 1.4 %unpack.1 = bf16[48,8,384]{2,1,0:T(8,128)(2,1)} custom-call(s32[48]{0:T(128)S(1)} %copy-done.6, bf16[16,6,8,384]{3,2,1,0:T(8,128)(2,1)S(1)} %all_to_all.10.back_ref), custom_call_target="tpu_custom_call" | custom-call | tf_op jit(solution)/shard_map/unpack/pallas_call | solution.py:498
Async XLA Ops:
  2.8 25.1 %all-to-all-start = ((bf16[16,19,8,128]{3,2,1,0:T(8,128)(2,1)}), bf16[16,19,8,128]{3,2,1,0:T(8,128)(2,1)S(1)}, u32[]{:S(2)}, u32[]{:S(2)}) async-start(bf16[16,19,8,128]{3,2,1,0:T(8,128)(2,1)} %pack.1), calls=%async_computation | async-start | bytes 1245184 | tf_op jit(solution)/shard_map/all_to_all | solution.py:383
  13.3 1.4 %copy-start = (bf16[384,3072]{1,0:T(8,128)(2,1)}, bf16[384,3072]{1,0:T(8,128)(2,1)S(1)}, u32[]{:S(2)}) copy-start(bf16[384,3072]{1,0:T(8,128)(2,1)S(1)} %get-tuple-element.16.far_hbm) | copy-start | bytes 7077892
  29.8 13.7 %copy-start.1 = (bf16[192,24]{1,0:T(8,128)(2,1)S(1)}, bf16[192,24]{1,0:T(8,128)(2,1)}, u32[]{:S(2)}) copy-start(bf16[192,24]{1,0:T(8,128)(2,1)} %constant.14.clone.refs_4_) | copy-start | bytes 27652
  29.9 13.7 %copy-start.2 = (bf16[192,24]{1,0:T(8,128)(2,1)S(1)}, bf16[192,24]{1,0:T(8,128)(2,1)}, u32[]{:S(2)}) copy-start(bf16[192,24]{1,0:T(8,128)(2,1)} %constant.13.clone.refs_3_) | copy-start | bytes 27652
  29.9 13.7 %copy-start.3 = (bf16[48,192]{1,0:T(8,128)(2,1)S(1)}, bf16[48,192]{1,0:T(8,128)(2,1)}, u32[]{:S(2)}) copy-start(bf16[48,192]{1,0:T(8,128)(2,1)} %constant.12.clone.refs_2_) | copy-start | bytes 55300
  29.9 13.7 %copy-start.4 = (bf16[48,192]{1,0:T(8,128)(2,1)S(1)}, bf16[48,192]{1,0:T(8,128)(2,1)}, u32[]{:S(2)}) copy-start(bf16[48,192]{1,0:T(8,128)(2,1)} %constant.11.clone.refs_1_) | copy-start | bytes 55300
  29.9 13.7 %copy-start.5 = (f32[16,192]{1,0:T(8,128)S(1)}, f32[16,192]{1,0:T(8,128)}, u32[]{:S(2)}) copy-start(f32[16,192]{1,0:T(8,128)} %constant.10.clone.refs_0_) | copy-start | bytes 36868
  31.4 3.7 %collective-permute-start.1 = (f32[16,192]{1,0:T(8,128)S(1)}, f32[16,192]{1,0:T(8,128)S(1)}, u32[]{:S(2)}, u32[]{:S(2)}) collective-permute-start(f32[16,192]{1,0:T(8,128)S(1)} %far.1.far_ref), channel_id=1, source_target_pairs={{0,2},{2,0},{4,6},{6,4},{1,3},{3,1},{5,7},{7,5},{8,10},{10,8},{12,... | collective-permute-start | bytes 36872 | tf_op jit(solution)/shard_map/ppermute | solution.py:441
  31.5 5.6 %collective-permute-start = (f32[16,192]{1,0:T(8,128)S(1)}, f32[16,192]{1,0:T(8,128)S(1)}, u32[]{:S(2)}, u32[]{:S(2)}) collective-permute-start(f32[16,192]{1,0:T(8,128)S(1)} %get-tuple-element.18.near_ref), channel_id=1, source_target_pairs={{0,6},{2,4},{4,2},{6,0},{1,7},{3,5},{5,3},{7,1},{8,14},{10,12},{12... | collective-permute-start | bytes 36872 | tf_op jit(solution)/shard_map/ppermute | solution.py:431
  37.1 6.4 %collective-permute-start.5 = (f32[16,768]{1,0:T(8,128)S(1)}, f32[16,768]{1,0:T(8,128)S(1)}, u32[]{:S(2)}, u32[]{:S(2)}) collective-permute-start(f32[16,768]{1,0:T(8,128)S(1)} %get-tuple-element.22.refs_6_), channel_id=1, source_target_pairs={{0,1},{1,0},{2,3},{3,2},{4,5},{5,4},{6,7},{7,6},{8,9},{9,8},{10,11... | collective-permute-start | bytes 147464 | tf_op jit(solution)/shard_map/ppermute | solution.py:323
  38.7 4.2 %collective-permute-start.4 = (f32[8,768]{1,0:T(8,128)S(1)}, f32[8,768]{1,0:T(8,128)S(1)}, u32[]{:S(2)}, u32[]{:S(2)}) collective-permute-start(f32[8,768]{1,0:T(8,128)S(1)} %get-tuple-element.21), channel_id=1, source_target_pairs={{0,9},{1,8},{8,17},{9,16},{16,25},{17,24},{24,1},{25,0},{2,11},{3,... | collective-permute-start | bytes 73736 | tf_op jit(solution)/shard_map/ppermute | solution.py:323
  38.7 4.2 %collective-permute-start.2 = (f32[8,768]{1,0:T(8,128)S(1)}, f32[8,768]{1,0:T(8,128)S(1)}, u32[]{:S(2)}, u32[]{:S(2)}) collective-permute-start(f32[8,768]{1,0:T(8,128)S(1)} %get-tuple-element.21), channel_id=1, source_target_pairs={{0,8},{1,9},{8,16},{9,17},{16,24},{17,25},{24,0},{25,1},{2,10},{3,... | collective-permute-start | bytes 73736 | tf_op jit(solution)/shard_map/ppermute | solution.py:323
  40.0 3.3 %collective-permute-start.6 = (f32[8,768]{1,0:T(8,128)S(1)}, f32[8,768]{1,0:T(8,128)S(1)}, u32[]{:S(2)}, u32[]{:S(2)}) collective-permute-start(f32[8,768]{1,0:T(8,128)S(1)} %get-tuple-element.23), channel_id=1, source_target_pairs={{0,25},{1,24},{8,1},{9,0},{16,9},{17,8},{24,17},{25,16},{2,27},{3,... | collective-permute-start | bytes 73736 | tf_op jit(solution)/shard_map/ppermute | solution.py:323
  41.3 2.2 %collective-permute-start.3 = (f32[8,768]{1,0:T(8,128)S(1)}, f32[8,768]{1,0:T(8,128)S(1)}, u32[]{:S(2)}, u32[]{:S(2)}) collective-permute-start(f32[8,768]{1,0:T(8,128)S(1)} %get-tuple-element.23), channel_id=1, source_target_pairs={{0,24},{1,25},{8,0},{9,1},{16,8},{17,9},{24,16},{25,17},{2,26},{3,... | collective-permute-start | bytes 73736 | tf_op jit(solution)/shard_map/ppermute | solution.py:323
  45.8 23.8 %copy-start.6 = (s32[48]{0:T(128)S(1)}, s32[48]{0:T(128)}, u32[]{:S(2)}) copy-start(s32[48]{0:T(128)} %tile_ref.1) | copy-start | bytes 580

commit v2 on v1

--- a/solution.py
+++ b/solution.py
@@ -60,8 +60,8 @@
 
 
 def pack_kernel(
-    capacity, chunks, empty, tile_hbm, place_hbm, slab_hbm, out_ref,
-    tile_ref, place_ref, slab_ref, count_ref, label_ref, sems,
+    capacity, chunks, empty, groups, tile_hbm, place_hbm, slab_hbm, out_hbm,
+    tile_ref, place_ref, slab_ref, count_ref, index_ref, label_ref, out_ref, sems, out_sems,
 ):
     copies = [
         pltpu.make_async_copy(tile_hbm, tile_ref, sems.at[0]),
@@ -72,19 +72,35 @@
         copy.start()
     tile_count = out_ref.shape[0]
     label_ref[...] = jnp.full(label_ref.shape, empty, jnp.float32)
-    out_ref[...] = jnp.zeros(out_ref.shape, out_ref.dtype)
-    for copy in copies:
+    for j in range(tile_count * capacity):
+        index_ref[j] = 0
+    for copy in copies[:2]:
         copy.wait()
 
-    def visit(i, t, slot):
-        slab = slab_ref[i]
-        for c in range(chunks):
-            out_ref[t, slot * chunks + c] = slab[:, c * LANES : (c + 1) * LANES]
+    def rank(i, t, slot):
+        index_ref[t * capacity + slot] = i
         label = place_ref[i].astype(jnp.float32)
         label_ref[t, pl.ds(slot, 1), :] = jnp.full((1, LANES), label, jnp.float32)
 
-    for_each_slab(tile_ref, count_ref, tile_count, slab_ref.shape[0], visit)
-    out_ref[:, capacity * chunks] = label_ref[...].astype(jnp.bfloat16)
+    for_each_slab(tile_ref, count_ref, tile_count, slab_ref.shape[0], rank)
+    copies[2].wait()
+
+    def fill(t, carry):
+        for k in range(capacity):
+            slab = slab_ref[index_ref[t * capacity + k]]
+            for c in range(chunks):
+                out_ref[t, k * chunks + c] = slab[:, c * LANES : (c + 1) * LANES]
+        out_ref[t, capacity * chunks] = label_ref[t].astype(jnp.bfloat16)
+        return carry
+
+    share = tile_count // groups
+    for g in range(groups):
+        lax.fori_loop(g * share, (g + 1) * share, fill, 0, unroll=min(share, 4))
+        part = slice(g * share, (g + 1) * share)
+        copies.append(pltpu.make_async_copy(out_ref.at[part], out_hbm.at[part], out_sems.at[g]))
+        copies[-1].start()
+    for copy in copies[3:]:
+        copy.wait()
 
 
 def odd_row():
@@ -116,7 +132,7 @@
     copy.wait()
 
 
-def arrange(capacity, chunks, arrived_ref, place_ref, wide_ref, turned_ref):
+def arrange(capacity, chunks, arrived_ref, place_ref, square_ref, last_ref, wide_ref, turned_ref):
     tile_count, _, rows, _ = arrived_ref.shape
     slots = tile_count * capacity
     labels = arrived_ref[:, capacity * chunks].astype(jnp.float32)[:, :capacity]
@@ -148,15 +164,33 @@
         across = wide_ref[...].T.astype(jnp.bfloat16)
         turned_ref[c * LANES : (c + 1) * LANES, :] = jnp.dot(
             across, hot, preferred_element_type=jnp.float32
-        ).astype(jnp.bfloat16)
-
-
-def half_density(piece, turned_ref, values_ref, out_ref):
+        )
+    size = square_ref.shape[0]
+    square_ref[...] = turned_ref[:size, :size].astype(jnp.bfloat16)
+    column = turned_ref[:size, size:] + turned_ref[size:, :size].T
+    high = column.astype(jnp.bfloat16)
+    last_ref[:size, :LANES] = high
+    last_ref[:size, LANES:] = (column - high.astype(jnp.float32)).astype(jnp.bfloat16)
+    last_ref[size:, :LANES] = turned_ref[size:, size:].astype(jnp.bfloat16)
+    last_ref[size:, LANES:] = jnp.zeros((LANES, LANES), jnp.bfloat16)
+
+
+def half_density(piece, square_ref, last_ref, values_ref, out_ref):
     half = out_ref.shape[1]
+    size = square_ref.shape[0]
     for q in range(values_ref.shape[1] // piece):
-        block = values_ref[:, q * piece : (q + 1) * piece]
-        mixed = jnp.dot(turned_ref[...], block, preferred_element_type=jnp.float32)
-        density = jnp.sum(mixed * block.astype(jnp.float32), axis=0, keepdims=True)
+        lanes = slice(q * piece, (q + 1) * piece)
+        block, end = values_ref[:size, lanes], values_ref[size:, lanes]
+        mixed = jnp.dot(
+            last_ref[...],
+            jnp.concatenate([end, end], axis=0),
+            preferred_element_type=jnp.float32,
+        )
+        inner = mixed[:size] + jnp.dot(
+            square_ref[...], block, preferred_element_type=jnp.float32
+        )
+        density = jnp.sum(inner * block.astype(jnp.float32), axis=0, keepdims=True)
+        density += jnp.sum(mixed[size:] * end.astype(jnp.float32), axis=0, keepdims=True)
         for p in range(piece // half):
             row = q * (piece // half) + p
             out_ref[row : row + 1, :] = density[:, p * half : (p + 1) * half]
@@ -164,17 +198,17 @@
 
 def near_kernel(
     capacity, chunks, piece, arrived_ref, near_ref, far_hbm,
-    out_ref, place_ref, turned_ref, far_ref, wide_ref, sem,
+    out_ref, place_ref, square_ref, last_ref, far_ref, wide_ref, turned_ref, sem,
 ):
     copy = pltpu.make_async_copy(far_hbm, far_ref, sem.at[0])
     copy.start()
-    arrange(capacity, chunks, arrived_ref, place_ref, wide_ref, turned_ref)
-    half_density(piece, turned_ref, near_ref, out_ref)
+    arrange(capacity, chunks, arrived_ref, place_ref, square_ref, last_ref, wide_ref, turned_ref)
+    half_density(piece, square_ref, last_ref, near_ref, out_ref)
     copy.wait()
 
 
-def far_kernel(piece, turned_ref, far_ref, out_ref):
-    half_density(piece, turned_ref, far_ref, out_ref)
+def far_kernel(piece, square_ref, last_ref, far_ref, out_ref):
+    half_density(piece, square_ref, last_ref, far_ref, out_ref)
 
 
 def join_kernel(near_ref, far_ref, wrap_ref, pair_ref, out_ref, top_ref, bottom_ref):
@@ -362,20 +396,23 @@
     plane = size_y * size_z
     counts = pltpu.SMEM((tile_count,), jnp.int32)
 
+    groups = math.gcd(tile_count, 4)
+    packed_shape = (tile_count, capacity * chunks + 1, atom_orb, LANES)
     packed = pl.pallas_call(
-        functools.partial(pack_kernel, capacity, chunks, float(list_blk)),
-        out_shape=jax.ShapeDtypeStruct(
-            (tile_count, capacity * chunks + 1, atom_orb, LANES), jnp.bfloat16
-        ),
+        functools.partial(pack_kernel, capacity, chunks, float(list_blk), groups),
+        out_shape=jax.ShapeDtypeStruct(packed_shape, jnp.bfloat16),
         in_specs=[HBM_SPEC] * 3,
-        out_specs=VMEM_SPEC,
+        out_specs=HBM_SPEC,
         scratch_shapes=[
             pltpu.SMEM((slab_count,), jnp.int32),
             pltpu.SMEM((slab_count,), jnp.int32),
             pltpu.VMEM(dm_slabs.shape, dm_slabs.dtype),
             counts,
+            pltpu.SMEM((tile_count * capacity,), jnp.int32),
             pltpu.VMEM((tile_count, atom_orb, LANES), jnp.float32),
+            pltpu.VMEM(packed_shape, jnp.bfloat16),
             pltpu.SemaphoreType.DMA((3,)),
+            pltpu.SemaphoreType.DMA((groups,)),
         ],
         compiler_params=grant(4),
         name="pack",
@@ -407,18 +444,20 @@
 
     slots = LANES * ((tile_count * capacity + LANES - 1) // LANES)
     product = 2 * half_points * list_orb * list_orb
-    near_y, places, matrix, far = pl.pallas_call(
+    near_y, places, square, last, far = pl.pallas_call(
         functools.partial(near_kernel, capacity, chunks, piece),
         out_shape=(
             f32(size_x, half),
             jax.ShapeDtypeStruct((1, slots), jnp.int32),
-            bf16(list_orb, list_orb),
+            bf16(list_orb - LANES, list_orb - LANES),
+            bf16(list_orb, 2 * LANES),
             pltpu.VMEM((list_orb, half_points), jnp.bfloat16),
         ),
         in_specs=[VMEM_SPEC, VMEM_SPEC, HBM_SPEC],
-        out_specs=(VMEM_SPEC,) * 4,
+        out_specs=(VMEM_SPEC,) * 5,
         scratch_shapes=[
             pltpu.VMEM((tile_count * capacity * atom_orb, LANES), jnp.float32),
+            pltpu.VMEM((list_orb, list_orb), jnp.float32),
             pltpu.SemaphoreType.DMA((1,)),
         ],
         compiler_params=grant(20),
@@ -432,12 +471,12 @@
     far_y = pl.pallas_call(
         functools.partial(far_kernel, piece),
         out_shape=f32(size_x, half),
-        in_specs=[VMEM_SPEC, VMEM_SPEC],
+        in_specs=[VMEM_SPEC] * 3,
         out_specs=VMEM_SPEC,
         compiler_params=grant(20),
         cost_estimate=cost(product, 2 * half_points * list_orb),
         name="far",
-    )(matrix, far)
+    )(square, last, far)
     from_pair = lax.ppermute(far_y, "gy", pair)
 
     wide = 2 * plane

time: 71.3 us -> 70.8 us (level)
  no operation moved by 1% of the time
where the time goes in v2:
time: 70.8 us; the launch traced here: 70.5 us
  blocking collectives  20.8 us (29%)
  waiting for transfers between devices  19.2 us (27%)
  Pallas kernels  14.9 us (21%)
  starting transfers between devices  13.4 us (19%)
  local copies, waits for them, and re-layouts  1.45 us (2%)
  between operations  0.76 us (1%)
    all_to_all x1, blocking collectives, local(): lax.all_to_all(returned, ('gx', 'gy'), split_axis=0, concat_axis=0, tiled...  20.8 us
    all_to_all x1, waiting for transfers between devices, local(): lax.all_to_all(packed, ('gx', 'gy'), split_axis=0, concat_axis=0, tiled=T...  13.2 us
    all_to_all x1, starting transfers between devices, local(): lax.all_to_all(packed, ('gx', 'gy'), split_axis=0, concat_axis=0, tiled=T...  7.43 us
    ppermute x5, starting transfers between devices, moved(): return lax.ppermute(block, axes, pairs)  4.86 us
    pallas_call x1, Pallas kernels, local(): pl.pallas_call(functools.partial(turn_kernel, size_x), out_shape=(pltpu.V...  3.07 us
    pallas_call x1, Pallas kernels, local(): pl.pallas_call(functools.partial(potential_kernel, capacity, float(tile_p...  2.93 us
    ppermute x1, waiting for transfers between devices, local(): from_pair = lax.ppermute(far_y, 'gy', pair)  2.65 us
    pallas_call x1, Pallas kernels, local(): pl.pallas_call(functools.partial(filter_kernel, parts), out_shape=(pltpu....  2.25 us
  transfers between devices with their start and end apart: 8, of which 6 were waited for; matrix products, arithmetic and copies ran while one was open for 0% of the time, Pallas kernels for 4%

profile of v2, /device:TPU:0, one launch (start us, length us, event | category | flops | bytes accessed | tf_op | source)
XLA Modules:
  0.0 70.5 jit_solution(12928842215369805264)
XLA Ops:
  0.6 1.9 %pack.1 = bf16[16,19,8,128]{3,2,1,0:T(8,128)(2,1)} custom-call(s32[48]{0:T(128)} %tile_ref.1, s32[48]{0:T(128)} %place_hbm.1, bf16[48,8,384]{2,1,0:T(8,128)(2,1)} %slab_hbm.1), custom_call_target="tpu_custom_call" | custom-call | tf_op jit(solution)/shard_map/pack/pallas_call | solution.py:401
  2.5 7.4 %all-to-all-start = ((bf16[16,19,8,128]{3,2,1,0:T(8,128)(2,1)}), bf16[16,19,8,128]{3,2,1,0:T(8,128)(2,1)S(1)}, u32[]{:S(2)}, u32[]{:S(2)}) async-start(bf16[16,19,8,128]{3,2,1,0:T(8,128)(2,1)} %pack.1), calls=%async_computation | async-start | bytes 1245184 | tf_op jit(solution)/shard_map/all_to_all | solution.py:420
  10.0 3.1 %turn.1 = (bf16[384,3072]{1,0:T(8,128)(2,1)S(1)}, bf16[384,3072]{1,0:T(8,128)(2,1)S(1)}) custom-call(bf16[6144,384]{1,0:T(8,128)(2,1)} %bitcast.1), custom_call_target="tpu_custom_call" | custom-call | bytes 9437184 | tf_op jit(solution)/shard_map/turn/pallas_call | solution.py:426
  13.0 0.0 copy-start
  13.1 1.4 %copy-done = bf16[384,3072]{1,0:T(8,128)(2,1)} copy-done((bf16[384,3072]{1,0:T(8,128)(2,1)}, bf16[384,3072]{1,0:T(8,128)(2,1)S(1)}, u32[]{:S(2)}) %copy-start) | copy-done | bytes 2359320
  14.5 13.2 %all-to-all-done.arrived_ref = bf16[16,19,8,128]{3,2,1,0:T(8,128)(2,1)S(1)} async-done(((bf16[16,19,8,128]{3,2,1,0:T(8,128)(2,1)}), bf16[16,19,8,128]{3,2,1,0:T(8,128)(2,1)S(1)}, u32[]{:S(2)}, u32[]{:S(2)}) %all-to-all-start) | async-done | bytes 622624 | tf_op jit(solution)/shard_map/all_to_all | solution.py:420
  27.6 1.9 %near.1 = (f32[16,192]{1,0:T(8,128)S(1)}, s32[1,128]{1,0:T(1,128)S(1)}, bf16[256,256]{1,0:T(8,128)(2,1)S(1)}, bf16[384,256]{1,0:T(8,128)(2,1)S(1)}, bf16[384,3072]{1,0:T(8,128)(2,1)S(1)}) custom-call(bf16[16,19,8,128]{3,2,1,0:T(8,128)(2,1)S(1)} %all-to-all-done.arrived_ref, bf16[384,3072]{1,0:T(8,128)(2,1)S(1)} %get-tuple-element.16.near_ref, ...), custom_call_target="tpu_custom_call" | custom-call | flops 905969664 | bytes 2359296 | tf_op jit(solution)/shard_map/near/pallas_call | solution.py:447
  29.5 0.0 copy-start.1
  29.6 0.0 copy-start.2
  29.6 0.0 copy-start.3
  29.6 0.0 copy-start.4
  29.6 0.0 copy-start.5
  29.6 1.3 %far.1.far_ref = f32[16,192]{1,0:T(8,128)S(1)} custom-call(bf16[256,256]{1,0:T(8,128)(2,1)S(1)} %get-tuple-element.20.square_ref, bf16[384,256]{1,0:T(8,128)(2,1)S(1)} %get-tuple-element.21.last_ref, bf16[384,3072]{1,0:T(8,128)(2,1)S(1)} %get-tuple-element.22.far_ref), custom_call_target="tpu_custom_call" | custom-call | flops 905969664 | bytes 2359296 | tf_op jit(solution)/shard_map/far/pallas_call | solution.py:471
  30.9 0.0 collective-permute-start.1
  31.0 1.1 %collective-permute-start = (f32[16,192]{1,0:T(8,128)S(1)}, f32[16,192]{1,0:T(8,128)S(1)}, u32[]{:S(2)}, u32[]{:S(2)}) collective-permute-start(f32[16,192]{1,0:T(8,128)S(1)} %get-tuple-element.19.near_ref), channel_id=1, source_target_pairs={{0,6},{2,4},{4,2},{6,0},{1,7},{3,5},{5,3},{7,1},{8,14},{10,12},{12... | collective-permute-start | bytes 36872 | tf_op jit(solution)/shard_map/ppermute | solution.py:470
  32.0 2.6 %collective-permute-done.1.pair_ref = f32[16,192]{1,0:T(8,128)S(1)} collective-permute-done((f32[16,192]{1,0:T(8,128)S(1)}, f32[16,192]{1,0:T(8,128)S(1)}, u32[]{:S(2)}, u32[]{:S(2)}) %collective-permute-start.1) | collective-permute-done | bytes 12320 | tf_op jit(solution)/shard_map/ppermute | solution.py:480
  34.7 1.9 %collective-permute-done.wrap_ref = f32[16,192]{1,0:T(8,128)S(1)} collective-permute-done((f32[16,192]{1,0:T(8,128)S(1)}, f32[16,192]{1,0:T(8,128)S(1)}, u32[]{:S(2)}, u32[]{:S(2)}) %collective-permute-start) | collective-permute-done | bytes 12320 | tf_op jit(solution)/shard_map/ppermute | solution.py:470
  36.6 0.1 join.1
  36.6 1.5 %collective-permute-start.5 = (f32[16,768]{1,0:T(8,128)S(1)}, f32[16,768]{1,0:T(8,128)S(1)}, u32[]{:S(2)}, u32[]{:S(2)}) collective-permute-start(f32[16,768]{1,0:T(8,128)S(1)} %get-tuple-element.24.refs_6_), channel_id=1, source_target_pairs={{0,1},{1,0},{2,3},{3,2},{4,5},{5,4},{6,7},{7,6},{8,9},{9,8},{10,11... | collective-permute-start | bytes 147464 | tf_op jit(solution)/shard_map/ppermute | solution.py:357
  38.2 0.0 collective-permute-start.4
  38.2 1.3 %collective-permute-start.2 = (f32[8,768]{1,0:T(8,128)S(1)}, f32[8,768]{1,0:T(8,128)S(1)}, u32[]{:S(2)}, u32[]{:S(2)}) collective-permute-start(f32[8,768]{1,0:T(8,128)S(1)} %get-tuple-element.23), channel_id=1, source_target_pairs={{0,8},{1,9},{8,16},{9,17},{16,24},{17,25},{24,0},{25,1},{2,10},{3,... | collective-permute-start | bytes 73736 | tf_op jit(solution)/shard_map/ppermute | solution.py:357
  39.5 1.4 %collective-permute-start.6 = (f32[8,768]{1,0:T(8,128)S(1)}, f32[8,768]{1,0:T(8,128)S(1)}, u32[]{:S(2)}, u32[]{:S(2)}) collective-permute-start(f32[8,768]{1,0:T(8,128)S(1)} %get-tuple-element.25), channel_id=1, source_target_pairs={{0,25},{1,24},{8,1},{9,0},{16,9},{17,8},{24,17},{25,16},{2,27},{3,... | collective-permute-start | bytes 73736 | tf_op jit(solution)/shard_map/ppermute | solution.py:357
  40.8 0.7 collective-permute-start.3
  41.5 0.8 %collective-permute-done.4.refs_8_ = f32[8,768]{1,0:T(8,128)S(1)} collective-permute-done((f32[8,768]{1,0:T(8,128)S(1)}, f32[8,768]{1,0:T(8,128)S(1)}, u32[]{:S(2)}, u32[]{:S(2)}) %collective-permute-start.4) | collective-permute-done | bytes 24608 | tf_op jit(solution)/shard_map/ppermute | solution.py:357
  42.3 0.0 collective-permute-done.2.refs_5_
  42.3 0.4 collective-permute-done.6.refs_10_
  42.7 0.3 collective-permute-done.3.refs_7_
  43.0 0.0 collective-permute-done.5.refs_9_
  43.0 0.0 copy-done.1
  43.0 0.0 copy-done.2
  43.0 0.0 copy-done.3
  43.0 0.0 copy-done.4
  43.0 0.0 copy-done.5
  43.1 2.2 %filter.1 = (f32[16,16,24]{2,1,0:T(8,128)S(1)}, f32[16,384]{1,0:T(8,128)S(1)}) custom-call(f32[16,192]{1,0:T(8,128)S(1)} %copy-done.5, bf16[48,192]{1,0:T(8,128)(2,1)S(1)} %copy-done.4, bf16[48,192]{1,0:T(8,128)(2,1)S(1)} %copy-done.3, bf16[192,24]{1,0:T(8,128)(2,1)S(1)} %copy-done.2, bf16[192,24]{1,0:T(8,128)(2,1)S(1)} %copy-done.1, ...), custom_call_target="tpu_custom_call" | custom-call | tf_op jit(solution)/shard_map/filter/pallas_call | solution.py:501
  45.3 0.0 copy-start.6
  45.3 2.9 %potential.1 = (bf16[16,6,8,384]{3,2,1,0:T(8,128)(2,1)S(1)}, f32[16,16,24]{2,1,0:T(8,128)}) custom-call(s32[1,128]{1,0:T(1,128)S(1)} %get-tuple-element.18.place_vmem, f32[16,16,24]{2,1,0:T(8,128)S(1)} %get-tuple-element.26.grid_ref, f32[16,384]{1,0:T(8,128)S(1)} %get-tuple-element.27.field_ref, bf16[384,3072]{1,0:T(8,128)(2,1)S(1)} %get-tuple-element.16.near_ref, ...), custom_call_target="tpu_custom_call" | custom-call | tf_op jit(solution)/shard_map/potential/pallas_call | solution.py:516
  48.3 20.8 %all_to_all.10.back_ref = bf16[16,6,8,384]{3,2,1,0:T(8,128)(2,1)S(1)} all-to-all(bf16[16,6,8,384]{3,2,1,0:T(8,128)(2,1)S(1)} %get-tuple-element.29), channel_id=1, replica_groups=mesh['gx'=4,'gy'=4,'gz'=2] {'gx','gy'}, dimensions={0} | all-to-all | bytes 1179648 | tf_op jit(solution)/shard_map/all_to_all | solution.py:536
  69.1 0.0 copy-done.6
  69.1 1.4 %unpack.1 = bf16[48,8,384]{2,1,0:T(8,128)(2,1)} custom-call(s32[48]{0:T(128)S(1)} %copy-done.6, bf16[16,6,8,384]{3,2,1,0:T(8,128)(2,1)S(1)} %all_to_all.10.back_ref), custom_call_target="tpu_custom_call" | custom-call | tf_op jit(solution)/shard_map/unpack/pallas_call | solution.py:537
Async XLA Ops:
  2.5 25.1 %all-to-all-start = ((bf16[16,19,8,128]{3,2,1,0:T(8,128)(2,1)}), bf16[16,19,8,128]{3,2,1,0:T(8,128)(2,1)S(1)}, u32[]{:S(2)}, u32[]{:S(2)}) async-start(bf16[16,19,8,128]{3,2,1,0:T(8,128)(2,1)} %pack.1), calls=%async_computation | async-start | bytes 1245184 | tf_op jit(solution)/shard_map/all_to_all | solution.py:420
  13.0 1.4 %copy-start = (bf16[384,3072]{1,0:T(8,128)(2,1)}, bf16[384,3072]{1,0:T(8,128)(2,1)S(1)}, u32[]{:S(2)}) copy-start(bf16[384,3072]{1,0:T(8,128)(2,1)S(1)} %get-tuple-element.17.far_hbm) | copy-start | bytes 7077892
  29.5 13.5 %copy-start.1 = (bf16[192,24]{1,0:T(8,128)(2,1)S(1)}, bf16[192,24]{1,0:T(8,128)(2,1)}, u32[]{:S(2)}) copy-start(bf16[192,24]{1,0:T(8,128)(2,1)} %constant.14.clone.refs_4_) | copy-start | bytes 27652
  29.6 13.5 %copy-start.2 = (bf16[192,24]{1,0:T(8,128)(2,1)S(1)}, bf16[192,24]{1,0:T(8,128)(2,1)}, u32[]{:S(2)}) copy-start(bf16[192,24]{1,0:T(8,128)(2,1)} %constant.13.clone.refs_3_) | copy-start | bytes 27652
  29.6 13.5 %copy-start.3 = (bf16[48,192]{1,0:T(8,128)(2,1)S(1)}, bf16[48,192]{1,0:T(8,128)(2,1)}, u32[]{:S(2)}) copy-start(bf16[48,192]{1,0:T(8,128)(2,1)} %constant.12.clone.refs_2_) | copy-start | bytes 55300
  29.6 13.5 %copy-start.4 = (bf16[48,192]{1,0:T(8,128)(2,1)S(1)}, bf16[48,192]{1,0:T(8,128)(2,1)}, u32[]{:S(2)}) copy-start(bf16[48,192]{1,0:T(8,128)(2,1)} %constant.11.clone.refs_1_) | copy-start | bytes 55300
  29.6 13.5 %copy-start.5 = (f32[16,192]{1,0:T(8,128)S(1)}, f32[16,192]{1,0:T(8,128)}, u32[]{:S(2)}) copy-start(f32[16,192]{1,0:T(8,128)} %constant.10.clone.refs_0_) | copy-start | bytes 36868
  30.9 3.7 %collective-permute-start.1 = (f32[16,192]{1,0:T(8,128)S(1)}, f32[16,192]{1,0:T(8,128)S(1)}, u32[]{:S(2)}, u32[]{:S(2)}) collective-permute-start(f32[16,192]{1,0:T(8,128)S(1)} %far.1.far_ref), channel_id=1, source_target_pairs={{0,2},{2,0},{4,6},{6,4},{1,3},{3,1},{5,7},{7,5},{8,10},{10,8},{12,... | collective-permute-start | bytes 36872 | tf_op jit(solution)/shard_map/ppermute | solution.py:480
  31.0 5.6 %collective-permute-start = (f32[16,192]{1,0:T(8,128)S(1)}, f32[16,192]{1,0:T(8,128)S(1)}, u32[]{:S(2)}, u32[]{:S(2)}) collective-permute-start(f32[16,192]{1,0:T(8,128)S(1)} %get-tuple-element.19.near_ref), channel_id=1, source_target_pairs={{0,6},{2,4},{4,2},{6,0},{1,7},{3,5},{5,3},{7,1},{8,14},{10,12},{12... | collective-permute-start | bytes 36872 | tf_op jit(solution)/shard_map/ppermute | solution.py:470
  36.6 6.4 %collective-permute-start.5 = (f32[16,768]{1,0:T(8,128)S(1)}, f32[16,768]{1,0:T(8,128)S(1)}, u32[]{:S(2)}, u32[]{:S(2)}) collective-permute-start(f32[16,768]{1,0:T(8,128)S(1)} %get-tuple-element.24.refs_6_), channel_id=1, source_target_pairs={{0,1},{1,0},{2,3},{3,2},{4,5},{5,4},{6,7},{7,6},{8,9},{9,8},{10,11... | collective-permute-start | bytes 147464 | tf_op jit(solution)/shard_map/ppermute | solution.py:357
  38.2 4.2 %collective-permute-start.4 = (f32[8,768]{1,0:T(8,128)S(1)}, f32[8,768]{1,0:T(8,128)S(1)}, u32[]{:S(2)}, u32[]{:S(2)}) collective-permute-start(f32[8,768]{1,0:T(8,128)S(1)} %get-tuple-element.23), channel_id=1, source_target_pairs={{0,9},{1,8},{8,17},{9,16},{16,25},{17,24},{24,1},{25,0},{2,11},{3,... | collective-permute-start | bytes 73736 | tf_op jit(solution)/shard_map/ppermute | solution.py:357
  38.2 4.2 %collective-permute-start.2 = (f32[8,768]{1,0:T(8,128)S(1)}, f32[8,768]{1,0:T(8,128)S(1)}, u32[]{:S(2)}, u32[]{:S(2)}) collective-permute-start(f32[8,768]{1,0:T(8,128)S(1)} %get-tuple-element.23), channel_id=1, source_target_pairs={{0,8},{1,9},{8,16},{9,17},{16,24},{17,25},{24,0},{25,1},{2,10},{3,... | collective-permute-start | bytes 73736 | tf_op jit(solution)/shard_map/ppermute | solution.py:357
  39.5 3.3 %collective-permute-start.6 = (f32[8,768]{1,0:T(8,128)S(1)}, f32[8,768]{1,0:T(8,128)S(1)}, u32[]{:S(2)}, u32[]{:S(2)}) collective-permute-start(f32[8,768]{1,0:T(8,128)S(1)} %get-tuple-element.25), channel_id=1, source_target_pairs={{0,25},{1,24},{8,1},{9,0},{16,9},{17,8},{24,17},{25,16},{2,27},{3,... | collective-permute-start | bytes 73736 | tf_op jit(solution)/shard_map/ppermute | solution.py:357
  40.8 2.2 %collective-permute-start.3 = (f32[8,768]{1,0:T(8,128)S(1)}, f32[8,768]{1,0:T(8,128)S(1)}, u32[]{:S(2)}, u32[]{:S(2)}) collective-permute-start(f32[8,768]{1,0:T(8,128)S(1)} %get-tuple-element.25), channel_id=1, source_target_pairs={{0,24},{1,25},{8,0},{9,1},{16,8},{17,9},{24,16},{25,17},{2,26},{3,... | collective-permute-start | bytes 73736 | tf_op jit(solution)/shard_map/ppermute | solution.py:357
  45.3 23.8 %copy-start.6 = (s32[48]{0:T(128)S(1)}, s32[48]{0:T(128)}, u32[]{:S(2)}) copy-start(s32[48]{0:T(128)} %tile_ref.1) | copy-start | bytes 580

commit v3 on v2

--- a/solution.py
+++ b/solution.py
@@ -66,8 +66,13 @@
     copies = [
         pltpu.make_async_copy(tile_hbm, tile_ref, sems.at[0]),
         pltpu.make_async_copy(place_hbm, place_ref, sems.at[1]),
-        pltpu.make_async_copy(slab_hbm, slab_ref, sems.at[2]),
     ]
+    slab_share = slab_ref.shape[0] // groups
+    for g in range(groups):
+        part = slice(g * slab_share, (g + 1) * slab_share)
+        copies.append(
+            pltpu.make_async_copy(slab_hbm.at[part], slab_ref.at[part], sems.at[2 + g])
+        )
     for copy in copies:
         copy.start()
     tile_count = out_ref.shape[0]
@@ -83,7 +88,9 @@
         label_ref[t, pl.ds(slot, 1), :] = jnp.full((1, LANES), label, jnp.float32)
 
     for_each_slab(tile_ref, count_ref, tile_count, slab_ref.shape[0], rank)
-    copies[2].wait()
+    for copy in copies[2:]:
+        copy.wait()
+    sent = []
 
     def fill(t, carry):
         for k in range(capacity):
@@ -97,9 +104,9 @@
     for g in range(groups):
         lax.fori_loop(g * share, (g + 1) * share, fill, 0, unroll=min(share, 4))
         part = slice(g * share, (g + 1) * share)
-        copies.append(pltpu.make_async_copy(out_ref.at[part], out_hbm.at[part], out_sems.at[g]))
-        copies[-1].start()
-    for copy in copies[3:]:
+        sent.append(pltpu.make_async_copy(out_ref.at[part], out_hbm.at[part], out_sems.at[g]))
+        sent[-1].start()
+    for copy in sent:
         copy.wait()
 
 
@@ -235,9 +242,9 @@
 
 
 def filter_kernel(parts, *refs):
-    taps_ref, band_high, band_low, fold_high, fold_low = refs[:5]
-    blocks = refs[5 : 5 + 3 * parts]
-    out_ref, field_ref, grid_ref, first_ref, second_ref, third_ref = refs[5 + 3 * parts :]
+    taps_ref, band_ref, fold_high, fold_low = refs[:4]
+    blocks = refs[4 : 4 + 3 * parts]
+    out_ref, field_ref, grid_ref, first_ref, second_ref, third_ref = refs[4 + 3 * parts :]
     size_x, size_y, size_z = out_ref.shape
     wide_y, wide_x, lanes = first_ref.shape
     for part in range(parts):
@@ -250,7 +257,13 @@
                 ]
             start += rows
     grid = grid_ref[...].reshape(wide_y * wide_x, parts * size_z)
-    first_ref[...] = split_dot(grid, band_high[...], band_low[...]).reshape(wide_y, wide_x, lanes)
+    high = grid.astype(jnp.bfloat16)
+    low = (grid - high.astype(jnp.float32)).astype(jnp.bfloat16)
+    first_ref[...] = jnp.dot(
+        jnp.concatenate([high, low, high], axis=1),
+        band_ref[...],
+        preferred_element_type=jnp.float32,
+    ).reshape(wide_y, wide_x, lanes)
 
     def tap(distance, rows):
         return jnp.broadcast_to(taps_ref[distance : distance + 1, :], (rows, lanes))
@@ -382,7 +395,9 @@
         low = (table - high.astype(np.float64)).astype(np.float32).astype(jnp.bfloat16)
         return [high, low]
 
-    return [taps.astype(np.float32), *split(np.concatenate(bands, axis=0)), *split(fold)]
+    band_high, band_low = split(np.concatenate(bands, axis=0))
+    stacked = np.concatenate([band_high, band_high, band_low], axis=0)
+    return [taps.astype(np.float32), stacked, *split(fold)]
 
 
 def local(orbital_values, dm_slabs, slab_tile, slab_place):
@@ -396,7 +411,7 @@
     plane = size_y * size_z
     counts = pltpu.SMEM((tile_count,), jnp.int32)
 
-    groups = math.gcd(tile_count, 4)
+    groups = math.gcd(math.gcd(tile_count, slab_count), 4)
     packed_shape = (tile_count, capacity * chunks + 1, atom_orb, LANES)
     packed = pl.pallas_call(
         functools.partial(pack_kernel, capacity, chunks, float(list_blk), groups),
@@ -411,7 +426,7 @@
             pltpu.SMEM((tile_count * capacity,), jnp.int32),
             pltpu.VMEM((tile_count, atom_orb, LANES), jnp.float32),
             pltpu.VMEM(packed_shape, jnp.bfloat16),
-            pltpu.SemaphoreType.DMA((3,)),
+            pltpu.SemaphoreType.DMA((2 + groups,)),
             pltpu.SemaphoreType.DMA((groups,)),
         ],
         compiler_params=grant(4),

time: 70.8 us -> 70.8 us (level)
    unnamed x14 -> x12, local copies, waits for them, and re-layouts: 1.45 us -> 1.45 us
where the time goes in v3:
time: 70.8 us; the launch traced here: 70.5 us
  blocking collectives  20.8 us (29%)
  waiting for transfers between devices  19.2 us (27%)
  Pallas kernels  15 us (21%)
  starting transfers between devices  13.4 us (19%)
  local copies, waits for them, and re-layouts  1.45 us (2%)
  between operations  0.75 us (1%)
    all_to_all x1, blocking collectives, local(): lax.all_to_all(returned, ('gx', 'gy'), split_axis=0, concat_axis=0, tiled...  20.8 us
    all_to_all x1, waiting for transfers between devices, local(): lax.all_to_all(packed, ('gx', 'gy'), split_axis=0, concat_axis=0, tiled=T...  13.2 us
    all_to_all x1, starting transfers between devices, local(): lax.all_to_all(packed, ('gx', 'gy'), split_axis=0, concat_axis=0, tiled=T...  7.43 us
    ppermute x5, starting transfers between devices, moved(): return lax.ppermute(block, axes, pairs)  4.85 us
    pallas_call x1, Pallas kernels, local(): pl.pallas_call(functools.partial(turn_kernel, size_x), out_shape=(pltpu.V...  3.07 us
    pallas_call x1, Pallas kernels, local(): pl.pallas_call(functools.partial(potential_kernel, capacity, float(tile_p...  2.93 us
    ppermute x1, waiting for transfers between devices, local(): from_pair = lax.ppermute(far_y, 'gy', pair)  2.65 us
    pallas_call x1, Pallas kernels, local(): pl.pallas_call(functools.partial(filter_kernel, parts), out_shape=(pltpu....  2.28 us
  transfers between devices with their start and end apart: 8, of which 6 were waited for; matrix products, arithmetic and copies ran while one was open for 0% of the time, Pallas kernels for 4%

profile of v3, /device:TPU:0, one launch (start us, length us, event | category | flops | bytes accessed | tf_op | source)
XLA Modules:
  0.0 70.5 jit_solution(12816050557013157509)
XLA Ops:
  0.6 1.9 %pack.1 = bf16[16,19,8,128]{3,2,1,0:T(8,128)(2,1)} custom-call(s32[48]{0:T(128)} %tile_ref.1, s32[48]{0:T(128)} %place_hbm.1, bf16[48,8,384]{2,1,0:T(8,128)(2,1)} %slab_hbm.1), custom_call_target="tpu_custom_call" | custom-call | tf_op jit(solution)/shard_map/pack/pallas_call | solution.py:416
  2.6 7.4 %all-to-all-start = ((bf16[16,19,8,128]{3,2,1,0:T(8,128)(2,1)}), bf16[16,19,8,128]{3,2,1,0:T(8,128)(2,1)S(1)}, u32[]{:S(2)}, u32[]{:S(2)}) async-start(bf16[16,19,8,128]{3,2,1,0:T(8,128)(2,1)} %pack.1), calls=%async_computation | async-start | bytes 1245184 | tf_op jit(solution)/shard_map/all_to_all | solution.py:435
  10.0 3.1 %turn.1 = (bf16[384,3072]{1,0:T(8,128)(2,1)S(1)}, bf16[384,3072]{1,0:T(8,128)(2,1)S(1)}) custom-call(bf16[6144,384]{1,0:T(8,128)(2,1)} %bitcast.1), custom_call_target="tpu_custom_call" | custom-call | bytes 9437184 | tf_op jit(solution)/shard_map/turn/pallas_call | solution.py:441
  13.1 0.0 copy-start
  13.1 1.4 %copy-done = bf16[384,3072]{1,0:T(8,128)(2,1)} copy-done((bf16[384,3072]{1,0:T(8,128)(2,1)}, bf16[384,3072]{1,0:T(8,128)(2,1)S(1)}, u32[]{:S(2)}) %copy-start) | copy-done | bytes 2359320
  14.5 13.2 %all-to-all-done.arrived_ref = bf16[16,19,8,128]{3,2,1,0:T(8,128)(2,1)S(1)} async-done(((bf16[16,19,8,128]{3,2,1,0:T(8,128)(2,1)}), bf16[16,19,8,128]{3,2,1,0:T(8,128)(2,1)S(1)}, u32[]{:S(2)}, u32[]{:S(2)}) %all-to-all-start) | async-done | bytes 622624 | tf_op jit(solution)/shard_map/all_to_all | solution.py:435
  27.7 1.9 %near.1 = (f32[16,192]{1,0:T(8,128)S(1)}, s32[1,128]{1,0:T(1,128)S(1)}, bf16[256,256]{1,0:T(8,128)(2,1)S(1)}, bf16[384,256]{1,0:T(8,128)(2,1)S(1)}, bf16[384,3072]{1,0:T(8,128)(2,1)S(1)}) custom-call(bf16[16,19,8,128]{3,2,1,0:T(8,128)(2,1)S(1)} %all-to-all-done.arrived_ref, bf16[384,3072]{1,0:T(8,128)(2,1)S(1)} %get-tuple-element.16.near_ref, ...), custom_call_target="tpu_custom_call" | custom-call | flops 905969664 | bytes 2359296 | tf_op jit(solution)/shard_map/near/pallas_call | solution.py:462
  29.6 0.0 copy-start.1
  29.6 0.0 copy-start.2
  29.6 0.0 copy-start.3
  29.6 0.0 copy-start.4
  29.6 1.3 %far.1.far_ref = f32[16,192]{1,0:T(8,128)S(1)} custom-call(bf16[256,256]{1,0:T(8,128)(2,1)S(1)} %get-tuple-element.20.square_ref, bf16[384,256]{1,0:T(8,128)(2,1)S(1)} %get-tuple-element.21.last_ref, bf16[384,3072]{1,0:T(8,128)(2,1)S(1)} %get-tuple-element.22.far_ref), custom_call_target="tpu_custom_call" | custom-call | flops 905969664 | bytes 2359296 | tf_op jit(solution)/shard_map/far/pallas_call | solution.py:486
  31.0 0.0 collective-permute-start.1
  31.0 1.1 %collective-permute-start = (f32[16,192]{1,0:T(8,128)S(1)}, f32[16,192]{1,0:T(8,128)S(1)}, u32[]{:S(2)}, u32[]{:S(2)}) collective-permute-start(f32[16,192]{1,0:T(8,128)S(1)} %get-tuple-element.19.near_ref), channel_id=1, source_target_pairs={{0,6},{2,4},{4,2},{6,0},{1,7},{3,5},{5,3},{7,1},{8,14},{10,12},{12... | collective-permute-start | bytes 36872 | tf_op jit(solution)/shard_map/ppermute | solution.py:485
  32.1 2.6 %collective-permute-done.1.pair_ref = f32[16,192]{1,0:T(8,128)S(1)} collective-permute-done((f32[16,192]{1,0:T(8,128)S(1)}, f32[16,192]{1,0:T(8,128)S(1)}, u32[]{:S(2)}, u32[]{:S(2)}) %collective-permute-start.1) | collective-permute-done | bytes 12320 | tf_op jit(solution)/shard_map/ppermute | solution.py:495
  34.7 1.9 %collective-permute-done.wrap_ref = f32[16,192]{1,0:T(8,128)S(1)} collective-permute-done((f32[16,192]{1,0:T(8,128)S(1)}, f32[16,192]{1,0:T(8,128)S(1)}, u32[]{:S(2)}, u32[]{:S(2)}) %collective-permute-start) | collective-permute-done | bytes 12320 | tf_op jit(solution)/shard_map/ppermute | solution.py:485
  36.6 0.1 join.1
  36.7 1.5 %collective-permute-start.5 = (f32[16,768]{1,0:T(8,128)S(1)}, f32[16,768]{1,0:T(8,128)S(1)}, u32[]{:S(2)}, u32[]{:S(2)}) collective-permute-start(f32[16,768]{1,0:T(8,128)S(1)} %get-tuple-element.24.refs_5_), channel_id=1, source_target_pairs={{0,1},{1,0},{2,3},{3,2},{4,5},{5,4},{6,7},{7,6},{8,9},{9,8},{10,11... | collective-permute-start | bytes 147464 | tf_op jit(solution)/shard_map/ppermute | solution.py:370
  38.2 0.0 collective-permute-start.4
  38.2 1.3 %collective-permute-start.2 = (f32[8,768]{1,0:T(8,128)S(1)}, f32[8,768]{1,0:T(8,128)S(1)}, u32[]{:S(2)}, u32[]{:S(2)}) collective-permute-start(f32[8,768]{1,0:T(8,128)S(1)} %get-tuple-element.23), channel_id=1, source_target_pairs={{0,8},{1,9},{8,16},{9,17},{16,24},{17,25},{24,0},{25,1},{2,10},{3,... | collective-permute-start | bytes 73736 | tf_op jit(solution)/shard_map/ppermute | solution.py:370
  39.5 1.4 %collective-permute-start.6 = (f32[8,768]{1,0:T(8,128)S(1)}, f32[8,768]{1,0:T(8,128)S(1)}, u32[]{:S(2)}, u32[]{:S(2)}) collective-permute-start(f32[8,768]{1,0:T(8,128)S(1)} %get-tuple-element.25), channel_id=1, source_target_pairs={{0,25},{1,24},{8,1},{9,0},{16,9},{17,8},{24,17},{25,16},{2,27},{3,... | collective-permute-start | bytes 73736 | tf_op jit(solution)/shard_map/ppermute | solution.py:370
  40.9 0.7 collective-permute-start.3
  41.5 0.8 %collective-permute-done.4.refs_7_ = f32[8,768]{1,0:T(8,128)S(1)} collective-permute-done((f32[8,768]{1,0:T(8,128)S(1)}, f32[8,768]{1,0:T(8,128)S(1)}, u32[]{:S(2)}, u32[]{:S(2)}) %collective-permute-start.4) | collective-permute-done | bytes 24608 | tf_op jit(solution)/shard_map/ppermute | solution.py:370
  42.4 0.0 collective-permute-done.2.refs_4_
  42.4 0.4 collective-permute-done.6.refs_9_
  42.8 0.3 collective-permute-done.3.refs_6_
  43.0 0.0 collective-permute-done.5.refs_8_
  43.1 0.0 copy-done.1
  43.1 0.0 copy-done.2
  43.1 0.0 copy-done.3
  43.1 0.0 copy-done.4
  43.1 2.3 %filter.1 = (f32[16,16,24]{2,1,0:T(8,128)S(1)}, f32[16,384]{1,0:T(8,128)S(1)}) custom-call(f32[16,192]{1,0:T(8,128)S(1)} %copy-done.4, bf16[144,192]{1,0:T(8,128)(2,1)S(1)} %copy-done.1, bf16[192,24]{1,0:T(8,128)(2,1)S(1)} %copy-done.3, bf16[192,24]{1,0:T(8,128)(2,1)S(1)} %copy-done.2, f32[8,768]{1,0:T(8,128)S(1)} %collective-permute-done.2.refs_4_, ...), custom_call_target="tpu_custom_call" | custom-call | tf_op jit(solution)/shard_map/filter/pallas_call | solution.py:516
  45.4 0.0 copy-start.5
  45.4 2.9 %potential.1 = (bf16[16,6,8,384]{3,2,1,0:T(8,128)(2,1)S(1)}, f32[16,16,24]{2,1,0:T(8,128)}) custom-call(s32[1,128]{1,0:T(1,128)S(1)} %get-tuple-element.18.place_vmem, f32[16,16,24]{2,1,0:T(8,128)S(1)} %get-tuple-element.26.grid_ref, f32[16,384]{1,0:T(8,128)S(1)} %get-tuple-element.27.field_ref, bf16[384,3072]{1,0:T(8,128)(2,1)S(1)} %get-tuple-element.16.near_ref, ...), custom_call_target="tpu_custom_call" | custom-call | tf_op jit(solution)/shard_map/potential/pallas_call | solution.py:531
  48.3 20.8 %all_to_all.10.back_ref = bf16[16,6,8,384]{3,2,1,0:T(8,128)(2,1)S(1)} all-to-all(bf16[16,6,8,384]{3,2,1,0:T(8,128)(2,1)S(1)} %get-tuple-element.29), channel_id=1, replica_groups=mesh['gx'=4,'gy'=4,'gz'=2] {'gx','gy'}, dimensions={0} | all-to-all | bytes 1179648 | tf_op jit(solution)/shard_map/all_to_all | solution.py:551
  69.1 0.0 copy-done.5
  69.1 1.4 %unpack.1 = bf16[48,8,384]{2,1,0:T(8,128)(2,1)} custom-call(s32[48]{0:T(128)S(1)} %copy-done.5, bf16[16,6,8,384]{3,2,1,0:T(8,128)(2,1)S(1)} %all_to_all.10.back_ref), custom_call_target="tpu_custom_call" | custom-call | tf_op jit(solution)/shard_map/unpack/pallas_call | solution.py:552
Async XLA Ops:
  2.6 25.1 %all-to-all-start = ((bf16[16,19,8,128]{3,2,1,0:T(8,128)(2,1)}), bf16[16,19,8,128]{3,2,1,0:T(8,128)(2,1)S(1)}, u32[]{:S(2)}, u32[]{:S(2)}) async-start(bf16[16,19,8,128]{3,2,1,0:T(8,128)(2,1)} %pack.1), calls=%async_computation | async-start | bytes 1245184 | tf_op jit(solution)/shard_map/all_to_all | solution.py:435
  13.1 1.4 %copy-start = (bf16[384,3072]{1,0:T(8,128)(2,1)}, bf16[384,3072]{1,0:T(8,128)(2,1)S(1)}, u32[]{:S(2)}) copy-start(bf16[384,3072]{1,0:T(8,128)(2,1)S(1)} %get-tuple-element.17.far_hbm) | copy-start | bytes 7077892
  29.6 13.5 %copy-start.1 = (bf16[144,192]{1,0:T(8,128)(2,1)S(1)}, bf16[144,192]{1,0:T(8,128)(2,1)}, u32[]{:S(2)}) copy-start(bf16[144,192]{1,0:T(8,128)(2,1)} %constant.9.clone.refs_1_) | copy-start | bytes 165892
  29.6 13.5 %copy-start.2 = (bf16[192,24]{1,0:T(8,128)(2,1)S(1)}, bf16[192,24]{1,0:T(8,128)(2,1)}, u32[]{:S(2)}) copy-start(bf16[192,24]{1,0:T(8,128)(2,1)} %constant.11.clone.refs_3_) | copy-start | bytes 27652
  29.6 13.4 %copy-start.3 = (bf16[192,24]{1,0:T(8,128)(2,1)S(1)}, bf16[192,24]{1,0:T(8,128)(2,1)}, u32[]{:S(2)}) copy-start(bf16[192,24]{1,0:T(8,128)(2,1)} %constant.10.clone.refs_2_) | copy-start | bytes 27652
  29.6 13.4 %copy-start.4 = (f32[16,192]{1,0:T(8,128)S(1)}, f32[16,192]{1,0:T(8,128)}, u32[]{:S(2)}) copy-start(f32[16,192]{1,0:T(8,128)} %constant.8.clone.refs_0_) | copy-start | bytes 36868
  31.0 3.7 %collective-permute-start.1 = (f32[16,192]{1,0:T(8,128)S(1)}, f32[16,192]{1,0:T(8,128)S(1)}, u32[]{:S(2)}, u32[]{:S(2)}) collective-permute-start(f32[16,192]{1,0:T(8,128)S(1)} %far.1.far_ref), channel_id=1, source_target_pairs={{0,2},{2,0},{4,6},{6,4},{1,3},{3,1},{5,7},{7,5},{8,10},{10,8},{12,... | collective-permute-start | bytes 36872 | tf_op jit(solution)/shard_map/ppermute | solution.py:495
  31.0 5.6 %collective-permute-start = (f32[16,192]{1,0:T(8,128)S(1)}, f32[16,192]{1,0:T(8,128)S(1)}, u32[]{:S(2)}, u32[]{:S(2)}) collective-permute-start(f32[16,192]{1,0:T(8,128)S(1)} %get-tuple-element.19.near_ref), channel_id=1, source_target_pairs={{0,6},{2,4},{4,2},{6,0},{1,7},{3,5},{5,3},{7,1},{8,14},{10,12},{12... | collective-permute-start | bytes 36872 | tf_op jit(solution)/shard_map/ppermute | solution.py:485
  36.7 6.4 %collective-permute-start.5 = (f32[16,768]{1,0:T(8,128)S(1)}, f32[16,768]{1,0:T(8,128)S(1)}, u32[]{:S(2)}, u32[]{:S(2)}) collective-permute-start(f32[16,768]{1,0:T(8,128)S(1)} %get-tuple-element.24.refs_5_), channel_id=1, source_target_pairs={{0,1},{1,0},{2,3},{3,2},{4,5},{5,4},{6,7},{7,6},{8,9},{9,8},{10,11... | collective-permute-start | bytes 147464 | tf_op jit(solution)/shard_map/ppermute | solution.py:370
  38.2 4.2 %collective-permute-start.4 = (f32[8,768]{1,0:T(8,128)S(1)}, f32[8,768]{1,0:T(8,128)S(1)}, u32[]{:S(2)}, u32[]{:S(2)}) collective-permute-start(f32[8,768]{1,0:T(8,128)S(1)} %get-tuple-element.23), channel_id=1, source_target_pairs={{0,9},{1,8},{8,17},{9,16},{16,25},{17,24},{24,1},{25,0},{2,11},{3,... | collective-permute-start | bytes 73736 | tf_op jit(solution)/shard_map/ppermute | solution.py:370
  38.2 4.2 %collective-permute-start.2 = (f32[8,768]{1,0:T(8,128)S(1)}, f32[8,768]{1,0:T(8,128)S(1)}, u32[]{:S(2)}, u32[]{:S(2)}) collective-permute-start(f32[8,768]{1,0:T(8,128)S(1)} %get-tuple-element.23), channel_id=1, source_target_pairs={{0,8},{1,9},{8,16},{9,17},{16,24},{17,25},{24,0},{25,1},{2,10},{3,... | collective-permute-start | bytes 73736 | tf_op jit(solution)/shard_map/ppermute | solution.py:370
  39.5 3.3 %collective-permute-start.6 = (f32[8,768]{1,0:T(8,128)S(1)}, f32[8,768]{1,0:T(8,128)S(1)}, u32[]{:S(2)}, u32[]{:S(2)}) collective-permute-start(f32[8,768]{1,0:T(8,128)S(1)} %get-tuple-element.25), channel_id=1, source_target_pairs={{0,25},{1,24},{8,1},{9,0},{16,9},{17,8},{24,17},{25,16},{2,27},{3,... | collective-permute-start | bytes 73736 | tf_op jit(solution)/shard_map/ppermute | solution.py:370
  40.9 2.2 %collective-permute-start.3 = (f32[8,768]{1,0:T(8,128)S(1)}, f32[8,768]{1,0:T(8,128)S(1)}, u32[]{:S(2)}, u32[]{:S(2)}) collective-permute-start(f32[8,768]{1,0:T(8,128)S(1)} %get-tuple-element.25), channel_id=1, source_target_pairs={{0,24},{1,25},{8,0},{9,1},{16,8},{17,9},{24,16},{25,17},{2,26},{3,... | collective-permute-start | bytes 73736 | tf_op jit(solution)/shard_map/ppermute | solution.py:370
  45.4 23.8 %copy-start.5 = (s32[48]{0:T(128)S(1)}, s32[48]{0:T(128)}, u32[]{:S(2)}) copy-start(s32[48]{0:T(128)} %tile_ref.1) | copy-start | bytes 580
